TPU v7x, 512 devices: a whole 4x4x16 slice. The times are simulated.
512 devices in a mesh: slab: 64 (over z_lo, x, core), grp: 8 (over z_hi, y).
Axes of the slice: x: 4, y: 4, z: 16 (z_hi: 2, z_lo: 8; z = z_hi * 8 + z_lo), core: 2. Of those that a mesh axis runs over, the one named last changes fastest.
Arguments:
- adj_out: float32 [5, 512, 256, 256], P(None, 'grp', 'slab'), may hold values from -6 to 6
- advect: bfloat16 [3, 512, 256, 256], P(None, 'grp', 'slab'), may hold values from -4 to 4
- viscosity: bfloat16 [512, 256, 256], P('grp', 'slab'), may hold values from 0.099609375 to 0.796875
- body_mask: int32 [512, 256, 256], P('grp', 'slab'), may hold values 0 or 1
- marker_x: int32 [2048], replicated, may hold values from 128 to 191
- marker_z: int32 [2048], replicated, may hold values from 0 to 255
- marker_y: int32 [2048], replicated, may hold values from 64 to 191
- drag_weight: float32 [2048], replicated, may hold values from -5 to 5
- inv_x: float32 [512, 512], P(None, 'grp'), may hold values from 0 to 1, as said below
- inv_y: float32 [256, 256], replicated, may hold values from 0 to 1, as said below
- inv_z: float32 [256, 256], replicated, may hold values from 0 to 1, as said below
Outputs:
- state_adjoint: float32 [5, 512, 256, 256], P(None, 'grp', 'slab')
Inputs may be any that keep to these rules, and one draw needn't show every extreme that they name: `inv_x`: entries of a given inverse. `inv_y`: entries of a given inverse. `inv_z`: entries of a given inverse.
All inputs are finite; a program needn't handle non-finite values. No bound on the sum of `body_mask` on one device may be relied on, other than what follows from the above.
Results may differ from a plain program's by a relative error of at most 0.0003.
Values sent between devices are 32-bit elements; how exact they have to be, the bound alone decides.
No kernel may reach another device: no remote copies, remote signals or barrier semaphores. Data moves between devices by JAX's collectives and lax.ppermute only.
A program may use at most 64 MiB of HBM per device.

v0:
```python
import functools

import jax
import jax.numpy as jnp
from jax import lax
from jax.experimental import pallas as pl
from jax.experimental.pallas import tpu as pltpu
from jax.sharding import Mesh, PartitionSpec as P


time_step = 0.08
highest = lax.Precision.HIGHEST
chips = ("zl", "xx", "zh", "yy")
slab = ("zl", "xx", "co")
grp = ("zh", "yy")
swap = [(0, 1), (1, 0)]


def parts(value):
    high = value.astype(jnp.bfloat16)
    return high, (value - high.astype(jnp.float32)).astype(jnp.bfloat16)


def product(left, right):
    dot = functools.partial(jnp.dot, preferred_element_type=jnp.float32)
    return dot(left[0], right[0]) + (dot(left[0], right[1]) + dot(left[1], right[0]))


def gather_ring(block, axis):
    count = lax.axis_size(axis)
    me = lax.axis_index(axis)
    out = jnp.zeros((count,) + block.shape, block.dtype)
    out = lax.dynamic_update_index_in_dim(out, block, me, 0)
    for hop in range(1, count):
        from_it = lax.ppermute(block, axis, [(i, (i + hop) % count) for i in range(count)])
        out = lax.dynamic_update_index_in_dim(out, from_it, (me - hop) % count, 0)
    return out


def inv_x_pair(inv_x):
    pieces = lax.axis_size("xx") * lax.axis_size("co")
    depth = inv_x.shape[0] // pieces
    mine = lax.dynamic_slice_in_dim(inv_x, lax.axis_index(("xx", "co")) * depth, depth, axis=0)
    theirs = lax.ppermute(mine, "zh", swap)
    low = lax.axis_index("zh") == 0
    return jnp.concatenate([jnp.where(low, mine, theirs), jnp.where(low, theirs, mine)], axis=1)


def whole_inv_x(pair):
    for axis in ("co", "xx", "yy"):
        pair = gather_ring(pair, axis)
    return pair.reshape(pair.shape[0], -1, pair.shape[-1])


def pushes(marker_x, marker_z, marker_y, drag_weight, x_rows, z_rows, y_cells):
    x_offset = lax.axis_index(grp) * x_rows
    z_offset = lax.axis_index(slab) * z_rows
    local_x = marker_x - x_offset
    local_z = marker_z - z_offset
    inside = (local_x >= 0) & (local_x < x_rows) & (local_z >= 0) & (local_z < z_rows)
    cell = jnp.where(inside, local_x * z_rows + local_z, -1)
    cells = lax.broadcasted_iota(jnp.int32, (x_rows * z_rows, 1), 0)
    here = (cells == cell[None, :]).astype(jnp.float32)
    lanes = lax.broadcasted_iota(jnp.int32, (1, y_cells), 1)
    weighted = jnp.where(marker_y[:, None] == lanes, drag_weight[:, None], 0.0)
    out = jnp.dot(here, weighted, precision=highest)
    return out.reshape(x_rows, z_rows, y_cells)


def z_weights(inv_z, z_rows):
    count = inv_z.shape[0]
    half = count // 2
    groups = half // z_rows
    core = lax.axis_index("co")

    def chosen(which):
        k = lax.broadcasted_iota(jnp.int32, (half, count), 0)
        z = lax.broadcasted_iota(jnp.int32, (half, count), 1)
        return (z == (k % groups) * (2 * z_rows) + which * z_rows + k // groups).astype(jnp.float32)

    mine = chosen(core)
    both = jnp.concatenate([mine, chosen(1 - core)], axis=0)
    picked = jnp.einsum("az,zw->aw", both, inv_z, precision=highest)
    return jnp.einsum("bw,aw->ba", mine, picked, precision=highest)


def solve_kernel(fields, own_ref, other_ref, wz_high, wz_low, ix_high, ix_low, out_ref, z_ref, edge_ref):
    rows = own_ref.shape[0] // 256
    out_rows = out_ref.shape[0] // 256
    lane = lax.broadcasted_iota(jnp.int32, (32, 128), 1)
    low_half = lane < 64

    def lines(ref, c):
        evens, odds = [None, None], [None, None]
        for pair in range(2):
            even, odd = [], []
            for q in range(4):
                at = q * rows + 2 * c + pair
                first = ref[pl.ds(at, 32, stride=8 * rows), :]
                second = ref[pl.ds(at + 4 * rows, 32, stride=8 * rows), :]
                even.append(jnp.where(low_half, first, pltpu.roll(second, 64, 1)))
                odd.append(jnp.where(low_half, pltpu.roll(first, 64, 1), second))
            evens[pair] = jnp.concatenate(even, axis=1)
            odds[pair] = jnp.concatenate(odd, axis=1)
        return jnp.concatenate([evens[0], odds[0], evens[1], odds[1]], axis=0)

    wz = wz_high[...], wz_low[...]
    for c in range(fields):
        both = jnp.concatenate([lines(own_ref, c), lines(other_ref, c)], axis=0)
        z_ref[pl.ds(c * 128, 128), :] = product(wz, parts(both))
    ix = ix_high[...], ix_low[...]
    edge_ref[...] = jnp.zeros_like(edge_ref)
    for c in range(fields):
        done = product(parts(z_ref[pl.ds(c * 128, 128), :]), ix)
        for pair in range(2):
            for q in range(4):
                two = [done[(2 * pair + i) * 32 : (2 * pair + i + 1) * 32, q * 128 : q * 128 + 128] for i in range(2)]
                at = q * out_rows + 2 * c + pair
                first = jnp.where(low_half, two[0], pltpu.roll(two[1], 64, 1))
                second = jnp.where(low_half, pltpu.roll(two[0], 64, 1), two[1])
                out_ref[pl.ds(at, 32, stride=8 * out_rows), :] = first
                out_ref[pl.ds(at + 4 * out_rows, 32, stride=8 * out_rows), :] = second
                for i in range(2):
                    k = c * 4 + 2 * pair + i
                    outer = pltpu.roll(two[i], 2 * k + 1, 1)
                    inner = pltpu.roll(two[i], (2 * k + 65) % 128, 1)
                    for target, value, spot in (
                        (q - 1, outer, 2 * k + 1),
                        (q + 4 + 1, outer, 2 * k),
                        (q + 4 - 1, inner, 2 * k + 1),
                        (q + 1, inner, 2 * k),
                    ):
                        if 0 <= target < 8:
                            edge_ref[target] = jnp.where(lane == spot, value, edge_ref[target])
    for g in range(8):
        out_ref[pl.ds(g * out_rows + out_rows - 1, 32, stride=8 * out_rows), :] = edge_ref[g]


vmem = pl.BlockSpec(memory_space=pltpu.VMEM)
params = pltpu.CompilerParams(vmem_limit_bytes=24 * 2**20)


def solve_lines(own, other, weights, fields):
    return pl.pallas_call(
        functools.partial(solve_kernel, fields),
        out_shape=jax.ShapeDtypeStruct((own.shape[0] + 256, 128), jnp.float32),
        in_specs=[vmem] * 6,
        out_specs=vmem,
        scratch_shapes=[pltpu.VMEM((fields * 128, 512), jnp.float32), pltpu.VMEM((8, 32, 128), jnp.float32)],
        compiler_params=params,
        cost_estimate=pl.CostEstimate(
            flops=fields * 128 * 512 * (512 + 256) * 6, bytes_accessed=8 * 2**20, transcendentals=0
        ),
    )(own, other, *weights)


def weights_kernel(wz_ref, ix_ref, wz_high, wz_low, ix_high, ix_low):
    wz_high[...], wz_low[...] = parts(wz_ref[...])
    for yy in range(4):
        for zh in range(2):
            j = zh * 4 + yy
            rows = jnp.concatenate([ix_ref[q, pl.ds(64 * j, 64), :] for q in range(4)], axis=1)
            at = pl.ds(64 * (2 * yy + zh), 64)
            ix_high[at, :], ix_low[at, :] = parts(rows)


def prepared(wz, ix):
    half = lambda shape: jax.ShapeDtypeStruct(shape, jnp.bfloat16)
    count = ix.shape[1]
    return pl.pallas_call(
        weights_kernel,
        out_shape=(half(wz.shape), half(wz.shape), half((count, count)), half((count, count))),
        in_specs=[vmem] * 2,
        out_specs=(vmem,) * 4,
        compiler_params=params,
        cost_estimate=pl.CostEstimate(flops=2**20, bytes_accessed=2 * 2**20, transcendentals=0),
    )(wz, ix)


def masked_kernel(fields, got_ref, mask_ref, masked_ref, low_ref, high_ref, edge_ref):
    rows = got_ref.shape[0] // 256
    for c in range(fields):
        for pair in range(2):
            both = got_ref[pl.ds(2 * c + pair, 256, stride=rows), :].T
            for i in range(2):
                z = 2 * pair + i
                cells = both[64 * i : 64 * i + 64] * mask_ref[z]
                masked_ref[c, z] = cells
                if z == 0:
                    low_ref[c] = cells
                if z == 3:
                    high_ref[c] = cells
    edge_ref[...] = got_ref[pl.ds(rows - 1, 256, stride=rows), :].T[: 8 * fields]


def masked_cells(got, mask, fields):
    z_rows, x_rows, y_cells = mask.shape
    cells = lambda *shape: jax.ShapeDtypeStruct(shape, jnp.float32)
    return pl.pallas_call(
        functools.partial(masked_kernel, fields),
        out_shape=(
            cells(fields, z_rows, x_rows, y_cells),
            cells(fields, x_rows, y_cells),
            cells(fields, x_rows, y_cells),
            cells(2 * fields * z_rows, y_cells),
        ),
        in_specs=[vmem] * 2,
        out_specs=(vmem,) * 4,
        compiler_params=params,
        cost_estimate=pl.CostEstimate(flops=2**20, bytes_accessed=3 * 2**20, transcendentals=0),
    )(got, mask)


def stencil_kernel(fields, masked_ref, edge_ref, rim_ref, below_ref, above_ref, flow_ref, thick_ref, out_ref):
    row = lax.broadcasted_iota(jnp.int32, (64, 256), 0)
    lane = lax.broadcasted_iota(jnp.int32, (64, 256), 1)
    for z in range(4):
        flow_x, flow_z, flow_y = (flow_ref[i, z] for i in range(3))
        thick = thick_ref[z]
        for c in range(fields):
            k = 2 * (c * 4 + z)
            v = masked_ref[c, z]
            first = edge_ref[k : k + 1, :] * rim_ref[z : z + 1, :]
            last = edge_ref[k + 1 : k + 2, :] * rim_ref[4 + z : 5 + z, :]
            x_less = jnp.where(row == 0, first, pltpu.roll(v, 1, 0))
            x_more = jnp.where(row == 63, last, pltpu.roll(v, 63, 0))
            y_less = jnp.where(lane == 0, 0.0, pltpu.roll(v, 1, 1))
            y_more = jnp.where(lane == 255, 0.0, pltpu.roll(v, 255, 1))
            z_less = below_ref[c] if z == 0 else masked_ref[c, z - 1]
            z_more = above_ref[c] if z == 3 else masked_ref[c, z + 1]
            laplace = x_more + x_less + z_more + z_less + y_more + y_less - 6.0 * v
            slopes = flow_x * (x_more - x_less) + flow_z * (z_more - z_less) + flow_y * (y_more - y_less)
            done = v + time_step * (0.5 * slopes + thick * laplace)
            for half in range(2):
                out_ref[pl.ds(c * 512 + half * 4 + z, 64, stride=8), :] = done[:, half * 128 : half * 128 + 128]


def stencil(masked, edges, rim, below, above, flow, thick):
    fields, z_rows, x_rows, y_cells = masked.shape
    out = pl.pallas_call(
        functools.partial(stencil_kernel, fields),
        out_shape=jax.ShapeDtypeStruct((fields * x_rows * z_rows * y_cells // 128, 128), jnp.float32),
        in_specs=[vmem] * 7,
        out_specs=vmem,
        compiler_params=params,
        cost_estimate=pl.CostEstimate(flops=2**23, bytes_accessed=5 * 2**20, transcendentals=0),
    )(masked, edges, rim, below, above, flow, thick)
    out = out.reshape(fields, x_rows, y_cells // 128, z_rows, 128)
    return out.transpose(0, 1, 3, 2, 4).reshape(fields, x_rows, z_rows, y_cells)


def before_and_after(head, tail, axes):
    count = lax.axis_size(axes)
    before = lax.ppermute(tail, axes, [(i, i + 1) for i in range(count - 1)])
    after = lax.ppermute(head, axes, [(i + 1, i) for i in range(count - 1)])
    return before, after


def transposed(sent):
    return lax.all_to_all(sent, chips, split_axis=0, concat_axis=0, tiled=True)


def body(
    adj_out,
    advect,
    viscosity,
    body_mask,
    marker_x,
    marker_z,
    marker_y,
    drag_weight,
    inv_x,
    inv_y,
    inv_z,
):
    fields, x_rows, z_rows, y_cells = adj_out.shape
    pair = inv_x_pair(inv_x)
    wz = z_weights(inv_z, z_rows)
    pushed = pushes(marker_x, marker_z, marker_y, drag_weight, x_rows, z_rows, y_cells)
    seeded = adj_out.at[0].add(pushed)
    ysolved = jnp.einsum("lm,cxzl->mczx", inv_y, seeded, precision=highest)
    pair, sent = lax.optimization_barrier((pair, ysolved.reshape(y_cells, fields * z_rows * x_rows)))
    got = transposed(sent).reshape(-1, 128)
    full_x = whole_inv_x(pair)
    weights = prepared(wz, full_x)
    mask = body_mask.astype(jnp.float32).transpose(1, 0, 2)
    rim = jnp.concatenate(before_and_after(mask[:, 0], mask[:, -1], grp), axis=0)
    flow = advect.astype(jnp.float32).transpose(0, 2, 1, 3)
    thick = viscosity.astype(jnp.float32).transpose(1, 0, 2)
    other = lax.ppermute(got, "co", swap)
    back = solve_lines(got, other, weights, fields)
    solved = transposed(back.reshape(y_cells, -1)).reshape(-1, 128)
    masked, low, high, edges = masked_cells(solved, mask, fields)
    below, above = before_and_after(low, high, slab)
    return stencil(masked, edges, rim, below, above, flow, thick)


def solution(mesh):
    fine = Mesh(mesh.devices.reshape(8, 4, 2, 2, 4), ("zl", "xx", "co", "zh", "yy"))
    field = P(None, grp, slab, None)
    in_specs = (field, field, P(grp, slab, None), P(grp, slab, None), P(), P(), P(), P(), P(None, grp), P(), P())

    return jax.shard_map(body, mesh=fine, in_specs=in_specs, out_specs=field, check_vma=False)
```

profile of v0, /device:TPU:7, one launch (start us, length us, event | category | flops | bytes accessed | tf_op | source)
XLA Modules:
  0.0 235.9 jit_solution(5383586044258517174)
XLA Ops:
  0.1 0.9 copy-done.6
  1.1 15.4 %collective-permute-start = (f32[64,64]{0,1:T(8,128)S(1)}, f32[64,64]{0,1:T(8,128)S(1)}, u32[]{:S(2)}, u32[]{:S(2)}) collective-permute-start(f32[64,64]{0,1:T(8,128)S(1)} %constant_dynamic-slice_fusion), channel_id=1, source_target_pairs={{0,4},{4,0},{1,5},{5,1},{2,6},{6,2},{3,7},{7,3},{8,12},{12,8},{9,1... | collective-permute-start | bytes 49160 | tf_op jit(solution)/shard_map/ppermute | solution.py:44
  16.6 1.6 fusion
  18.4 1.2 fusion.2
  19.8 2.1 copy.30
  21.8 18.3 %all-to-all-start = ((f32[256,1,1280]{2,1,0:T(1,128)}), f32[256,1,1280]{2,1,0:T(1,128)S(1)}, u32[]{:S(2)}, u32[]{:S(2)}) async-start(f32[256,1,1280]{2,1,0:T(1,128)} %copy.30), calls=%async_computation | async-start | bytes 2621440 | tf_op jit(solution)/shard_map/all_to_all | solution.py:260
  41.1 4.1 %collective-permute-start.2 = (f32[64,128]{0,1:T(8,128)S(1)}, f32[64,128]{0,1:T(8,128)S(1)}, u32[]{:S(2)}, u32[]{:S(2)}) collective-permute-start(f32[64,128]{0,1:T(8,128)S(1)} %pad_maximum_fusion), channel_id=1, source_target_pairs={{0,8},{8,0},{1,9},{9,1},{2,10},{10,2},{3,11},{11,3},{4,12},{12,4},... | collective-permute-start | bytes 98312 | tf_op jit(solution)/shard_map/ppermute | solution.py:35
  45.3 0.8 collective-permute-done.2
  46.1 3.4 %collective-permute-start.3 = (f32[2,64,128]{2,1,0:T(8,128)S(1)}, f32[2,64,128]{2,1,0:T(8,128)S(1)}, u32[]{:S(2)}, u32[]{:S(2)}) collective-permute-start(f32[2,64,128]{2,1,0:T(8,128)S(1)} %constant_dynamic-update-slice_fusion), channel_id=1, source_target_pairs={{0,16},{16,32},{32,48},{48,0},{1,17},{17,33},{33,49},{49,1},{2,18}... | collective-permute-start | bytes 196616 | tf_op jit(solution)/shard_map/ppermute | solution.py:35
  49.5 2.8 %collective-permute-start.4 = (f32[2,64,128]{2,1,0:T(8,128)S(1)}, f32[2,64,128]{2,1,0:T(8,128)S(1)}, u32[]{:S(2)}, u32[]{:S(2)}) collective-permute-start(f32[2,64,128]{2,1,0:T(8,128)S(1)} %constant_dynamic-update-slice_fusion), channel_id=1, source_target_pairs={{0,32},{16,48},{32,0},{48,16},{1,33},{17,49},{33,1},{49,17},{2,34}... | collective-permute-start | bytes 196616 | tf_op jit(solution)/shard_map/ppermute | solution.py:35
  52.3 1.9 collective-permute-start.5
  54.3 2.3 collective-permute-done.4
  56.6 46.6 %all-to-all-done = f32[256,1,1280]{2,1,0:T(1,128)S(1)} async-done(((f32[256,1,1280]{2,1,0:T(1,128)}), f32[256,1,1280]{2,1,0:T(1,128)S(1)}, u32[]{:S(2)}, u32[]{:S(2)}) %all-to-all-start) | async-done | bytes 1310752 | tf_op jit(solution)/shard_map/all_to_all | solution.py:260
  103.2 5.6 %collective-permute-start.1 = (f32[2560,128]{1,0:T(8,128)S(1)}, f32[2560,128]{1,0:T(8,128)S(1)}, u32[]{:S(2)}, u32[]{:S(2)}) collective-permute-start(f32[2560,128]{1,0:T(8,128)S(1)} %bitcast.50), channel_id=1, source_target_pairs={{0,8},{8,0},{1,9},{9,1},{2,10},{10,2},{3,11},{11,3},{4,12},{12,4},... | collective-permute-start | bytes 3932168 | tf_op jit(solution)/shard_map/ppermute | solution.py:290
  108.8 1.9 collective-permute-start.6
  110.7 1.0 fusion.17.wz_ref
  111.8 2.3 collective-permute-start.7
  114.0 4.4 %collective-permute-start.8 = (f32[4,2,64,128]{3,2,1,0:T(8,128)S(1)}, f32[4,2,64,128]{3,2,1,0:T(8,128)S(1)}, u32[]{:S(2)}, u32[]{:S(2)}) collective-permute-start(f32[4,2,64,128]{3,2,1,0:T(8,128)S(1)} %bitcast_dynamic-update-slice_fusion.4), channel_id=1, source_target_pairs={{0,3},{1,0},{2,1},{3,2},{4,7},{5,4},{6,5},{7,6},{8,11},{9,8},{10,9... | collective-permute-start | bytes 786440 | tf_op jit(solution)/shard_map/ppermute | solution.py:35
  118.6 6.8 %collective-permute-done.6 = f32[4,2,64,128]{3,2,1,0:T(8,128)} collective-permute-done((f32[4,2,64,128]{3,2,1,0:T(8,128)S(1)}, f32[4,2,64,128]{3,2,1,0:T(8,128)}, u32[]{:S(2)}, u32[]{:S(2)}) %collective-permute-start.6) | collective-permute-done | bytes 262176 | tf_op jit(solution)/shard_map/ppermute | solution.py:35
  125.4 1.0 bitcast_dynamic-update-slice_fusion.2
  126.5 2.2 collective-permute-done.8
  128.8 4.0 %shard_map.110 = f32[2816,128]{1,0:T(8,128)} custom-call(f32[2560,128]{1,0:T(8,128)S(1)} %bitcast.51, f32[2560,128]{1,0:T(8,128)S(1)} %collective-permute-done.1.other_ref, bf16[128,256]{1,0:T(8,128)(2,1)S(1)} %get-tuple-element.29.wz_high, bf16[128,256]{1,0:T(8,128)(2,1)S(1)} %get-tuple-element.30.wz_low, bf16[512,512]{1,0:T(8,128)(2,1)S(1)} %get-tuple-element.31.ix_high, ...), custom_call_target="tpu_custom_call" | custom-call | flops 1509949440 | bytes 8388608 | tf_op jit(solution)/shard_map/pallas_call | solution.py:144
  132.8 13.3 %all-to-all-start.1 = ((f32[256,1,1408]{2,1,0:T(1,128)}), f32[256,1,1408]{2,1,0:T(1,128)S(1)}, u32[]{:S(2)}, u32[]{:S(2)}) async-start(f32[256,1,1408]{2,1,0:T(1,128)} %bitcast.17), calls=%async_computation.1 | async-start | bytes 2883584 | tf_op jit(solution)/shard_map/all_to_all | solution.py:260
  146.2 1.3 collective-permute-start.10
  147.5 4.0 %collective-permute-start.9 = (f32[4,256]{1,0:T(4,128)S(1)}, f32[4,256]{1,0:T(4,128)S(1)}, u32[]{:S(2)}, u32[]{:S(2)}) collective-permute-start(f32[4,256]{1,0:T(4,128)S(1)} %get-tuple-element.37), channel_id=1, source_target_pairs={{0,1},{1,2},{2,3},{3,4},{4,5},{5,6},{6,7},{8,9},{9,10},{10,11},{11... | collective-permute-start | bytes 12296 | tf_op jit(solution)/shard_map/ppermute | solution.py:254
  151.7 63.6 %all-to-all-done.1 = f32[256,1,1408]{2,1,0:T(1,128)S(1)} async-done(((f32[256,1,1408]{2,1,0:T(1,128)}), f32[256,1,1408]{2,1,0:T(1,128)S(1)}, u32[]{:S(2)}, u32[]{:S(2)}) %all-to-all-start.1) | async-done | bytes 1441824 | tf_op jit(solution)/shard_map/all_to_all | solution.py:260
  215.3 0.4 shard_map.111
  215.7 7.2 %collective-permute-start.11 = (f32[5,64,256]{2,1,0:T(8,128)S(1)}, f32[5,64,256]{2,1,0:T(8,128)S(1)}, u32[]{:S(2)}, u32[]{:S(2)}) collective-permute-start(f32[5,64,256]{2,1,0:T(8,128)S(1)} %get-tuple-element.35), channel_id=1, source_target_pairs={{0,8},{8,16},{16,24},{24,32},{32,40},{40,48},{48,56},{56,64},{64,7... | collective-permute-start | bytes 983048 | tf_op jit(solution)/shard_map/ppermute | solution.py:254
  223.0 1.9 collective-permute-start.12
  225.0 2.0 collective-permute-done.11.below_ref
  227.0 6.5 %collective-permute-done.12.above_ref = f32[5,64,256]{2,1,0:T(8,128)S(1)} collective-permute-done((f32[5,64,256]{2,1,0:T(8,128)S(1)}, f32[5,64,256]{2,1,0:T(8,128)S(1)}, u32[]{:S(2)}, u32[]{:S(2)}) %collective-permute-start.12) | collective-permute-done | bytes 327712 | tf_op jit(solution)/shard_map/ppermute | solution.py:255
  233.5 2.4 %shard_map.112 = f32[2560,128]{1,0:T(8,128)} custom-call(f32[5,4,64,256]{3,2,1,0:T(8,128)S(1)} %get-tuple-element.33.masked_ref, f32[40,256]{1,0:T(8,128)S(1)} %get-tuple-element.34.edge_ref, f32[8,256]{1,0:T(8,128)S(1)} %pad_maximum_fusion.1.rim_ref, f32[5,64,256]{2,1,0:T(8,128)S(1)} %collective-permute-done.11.below_ref, ...), custom_call_target="tpu_custom_call" | custom-call | flops 8388608 | bytes 5242880 | tf_op jit(solution)/shard_map/pallas_call | solution.py:240
  (64 shorter events, 2.0 us)
Async XLA Ops:
  0.0 18.4 %copy-start = (f32[256,256]{1,0:T(8,128)S(1)}, f32[256,256]{1,0:T(8,128)}, u32[]{:S(2)}) copy-start(f32[256,256]{1,0:T(8,128)} %param.22) | copy-start | bytes 786436
  0.0 16.5 %copy-start.8 = (s32[2048]{0:T(1024)S(1)}, s32[2048]{0:T(1024)}, u32[]{:S(2)}) copy-start(s32[2048]{0:T(1024)} %param.17) | copy-start | bytes 24580
  0.0 16.5 %copy-start.7 = (s32[2048]{0:T(1024)S(1)}, s32[2048]{0:T(1024)}, u32[]{:S(2)}) copy-start(s32[2048]{0:T(1024)} %param.18) | copy-start | bytes 24580
  0.0 16.5 %copy-start.12 = (s32[2048]{0:T(1024)S(1)}, s32[2048]{0:T(1024)}, u32[]{:S(2)}) copy-start(s32[2048]{0:T(1024)} %param.19) | copy-start | bytes 24580
  0.0 16.5 %copy-start.11 = (f32[2048]{0:T(1024)S(1)}, f32[2048]{0:T(1024)}, u32[]{:S(2)}) copy-start(f32[2048]{0:T(1024)} %param.20) | copy-start | bytes 24580
  0.0 0.9 copy-start.6
  1.1 18.6 %collective-permute-start = (f32[64,64]{0,1:T(8,128)S(1)}, f32[64,64]{0,1:T(8,128)S(1)}, u32[]{:S(2)}, u32[]{:S(2)}) collective-permute-start(f32[64,64]{0,1:T(8,128)S(1)} %constant_dynamic-slice_fusion), channel_id=1, source_target_pairs={{0,4},{4,0},{1,5},{5,1},{2,6},{6,2},{3,7},{7,3},{8,12},{12,8},{9,1... | collective-permute-start | bytes 49160 | tf_op jit(solution)/shard_map/ppermute | solution.py:44
  16.6 1.8 copy-start.1
  21.8 19.0 %copy-start.3 = (f32[256,256]{1,0:T(8,128)S(1)}, f32[256,256]{1,0:T(8,128)}, u32[]{:S(2)}) copy-start(f32[256,256]{1,0:T(8,128)} %param.23) | copy-start | bytes 786436
  21.8 81.3 %all-to-all-start = ((f32[256,1,1280]{2,1,0:T(1,128)}), f32[256,1,1280]{2,1,0:T(1,128)S(1)}, u32[]{:S(2)}, u32[]{:S(2)}) async-start(f32[256,1,1280]{2,1,0:T(1,128)} %copy.30), calls=%async_computation | async-start | bytes 2621440 | tf_op jit(solution)/shard_map/all_to_all | solution.py:260
  40.2 0.5 copy-start.9
  40.2 0.6 copy-start.10
  41.1 4.9 %collective-permute-start.2 = (f32[64,128]{0,1:T(8,128)S(1)}, f32[64,128]{0,1:T(8,128)S(1)}, u32[]{:S(2)}, u32[]{:S(2)}) collective-permute-start(f32[64,128]{0,1:T(8,128)S(1)} %pad_maximum_fusion), channel_id=1, source_target_pairs={{0,8},{8,0},{1,9},{9,1},{2,10},{10,2},{3,11},{11,3},{4,12},{12,4},... | collective-permute-start | bytes 98312 | tf_op jit(solution)/shard_map/ppermute | solution.py:35
  46.1 8.1 %collective-permute-start.3 = (f32[2,64,128]{2,1,0:T(8,128)S(1)}, f32[2,64,128]{2,1,0:T(8,128)S(1)}, u32[]{:S(2)}, u32[]{:S(2)}) collective-permute-start(f32[2,64,128]{2,1,0:T(8,128)S(1)} %constant_dynamic-update-slice_fusion), channel_id=1, source_target_pairs={{0,16},{16,32},{32,48},{48,0},{1,17},{17,33},{33,49},{49,1},{2,18}... | collective-permute-start | bytes 196616 | tf_op jit(solution)/shard_map/ppermute | solution.py:35
  49.5 7.1 %collective-permute-start.4 = (f32[2,64,128]{2,1,0:T(8,128)S(1)}, f32[2,64,128]{2,1,0:T(8,128)S(1)}, u32[]{:S(2)}, u32[]{:S(2)}) collective-permute-start(f32[2,64,128]{2,1,0:T(8,128)S(1)} %constant_dynamic-update-slice_fusion), channel_id=1, source_target_pairs={{0,32},{16,48},{32,0},{48,16},{1,33},{17,49},{33,1},{49,17},{2,34}... | collective-permute-start | bytes 196616 | tf_op jit(solution)/shard_map/ppermute | solution.py:35
  52.3 56.4 %collective-permute-start.5 = (f32[2,64,128]{2,1,0:T(8,128)S(1)}, f32[2,64,128]{2,1,0:T(8,128)S(1)}, u32[]{:S(2)}, u32[]{:S(2)}) collective-permute-start(f32[2,64,128]{2,1,0:T(8,128)S(1)} %constant_dynamic-update-slice_fusion), channel_id=1, source_target_pairs={{0,48},{16,0},{32,16},{48,32},{1,49},{17,1},{33,17},{49,33},{2,50}... | collective-permute-start | bytes 196616 | tf_op jit(solution)/shard_map/ppermute | solution.py:35
  103.2 25.7 %collective-permute-start.1 = (f32[2560,128]{1,0:T(8,128)S(1)}, f32[2560,128]{1,0:T(8,128)S(1)}, u32[]{:S(2)}, u32[]{:S(2)}) collective-permute-start(f32[2560,128]{1,0:T(8,128)S(1)} %bitcast.50), channel_id=1, source_target_pairs={{0,8},{8,0},{1,9},{9,1},{2,10},{10,2},{3,11},{11,3},{4,12},{12,4},... | collective-permute-start | bytes 3932168 | tf_op jit(solution)/shard_map/ppermute | solution.py:290
  108.8 16.7 %collective-permute-start.6 = (f32[4,2,64,128]{3,2,1,0:T(8,128)S(1)}, f32[4,2,64,128]{3,2,1,0:T(8,128)}, u32[]{:S(2)}, u32[]{:S(2)}) collective-permute-start(f32[4,2,64,128]{3,2,1,0:T(8,128)S(1)} %bitcast_dynamic-update-slice_fusion.4), channel_id=1, source_target_pairs={{0,1},{1,2},{2,3},{3,0},{4,5},{5,6},{6,7},{7,4},{8,9},{9,10},{10,1... | collective-permute-start | bytes 786440 | tf_op jit(solution)/shard_map/ppermute | solution.py:35
  111.8 14.7 %collective-permute-start.7 = (f32[4,2,64,128]{3,2,1,0:T(8,128)S(1)}, f32[4,2,64,128]{3,2,1,0:T(8,128)S(1)}, u32[]{:S(2)}, u32[]{:S(2)}) collective-permute-start(f32[4,2,64,128]{3,2,1,0:T(8,128)S(1)} %bitcast_dynamic-update-slice_fusion.4), channel_id=1, source_target_pairs={{0,2},{1,3},{2,0},{3,1},{4,6},{5,7},{6,4},{7,5},{8,10},{9,11},{10,... | collective-permute-start | bytes 786440 | tf_op jit(solution)/shard_map/ppermute | solution.py:35
  114.0 14.6 %collective-permute-start.8 = (f32[4,2,64,128]{3,2,1,0:T(8,128)S(1)}, f32[4,2,64,128]{3,2,1,0:T(8,128)S(1)}, u32[]{:S(2)}, u32[]{:S(2)}) collective-permute-start(f32[4,2,64,128]{3,2,1,0:T(8,128)S(1)} %bitcast_dynamic-update-slice_fusion.4), channel_id=1, source_target_pairs={{0,3},{1,0},{2,1},{3,2},{4,7},{5,4},{6,5},{7,6},{8,11},{9,8},{10,9... | collective-permute-start | bytes 786440 | tf_op jit(solution)/shard_map/ppermute | solution.py:35
  132.8 13.3 %copy-start.4 = (s32[64,4,256]{2,1,0:T(4,128)S(1)}, s32[64,4,256]{2,1,0:T(4,128)}, u32[]{:S(2)}) copy-start(s32[64,4,256]{2,1,0:T(4,128)} %param.16) | copy-start | bytes 786436
  132.8 18.8 %copy-start.2 = (bf16[3,64,4,256]{3,2,1,0:T(4,128)(2,1)S(1)}, bf16[3,64,4,256]{3,2,1,0:T(4,128)(2,1)}, u32[]{:S(2)}) copy-start(bf16[3,64,4,256]{3,2,1,0:T(4,128)(2,1)} %param.14) | copy-start | bytes 1179652
  132.8 82.5 %all-to-all-start.1 = ((f32[256,1,1408]{2,1,0:T(1,128)}), f32[256,1,1408]{2,1,0:T(1,128)S(1)}, u32[]{:S(2)}, u32[]{:S(2)}) async-start(f32[256,1,1408]{2,1,0:T(1,128)} %bitcast.17), calls=%async_computation.1 | async-start | bytes 2883584 | tf_op jit(solution)/shard_map/all_to_all | solution.py:260
  146.2 78.7 %collective-permute-start.10 = (f32[4,256]{1,0:T(4,128)S(1)}, f32[4,256]{1,0:T(4,128)S(1)}, u32[]{:S(2)}, u32[]{:S(2)}) collective-permute-start(f32[4,256]{1,0:T(4,128)S(1)} %get-tuple-element.38), channel_id=1, source_target_pairs={{1,0},{2,1},{3,2},{4,3},{5,4},{6,5},{7,6},{9,8},{10,9},{11,10},{12... | collective-permute-start | bytes 12296 | tf_op jit(solution)/shard_map/ppermute | solution.py:255
  147.5 77.4 %collective-permute-start.9 = (f32[4,256]{1,0:T(4,128)S(1)}, f32[4,256]{1,0:T(4,128)S(1)}, u32[]{:S(2)}, u32[]{:S(2)}) collective-permute-start(f32[4,256]{1,0:T(4,128)S(1)} %get-tuple-element.37), channel_id=1, source_target_pairs={{0,1},{1,2},{2,3},{3,4},{4,5},{5,6},{6,7},{8,9},{9,10},{10,11},{11... | collective-permute-start | bytes 12296 | tf_op jit(solution)/shard_map/ppermute | solution.py:254
  151.6 73.3 %copy-start.5 = (bf16[64,4,256]{2,1,0:T(4,128)(2,1)S(1)}, bf16[64,4,256]{2,1,0:T(4,128)(2,1)}, u32[]{:S(2)}) copy-start(bf16[64,4,256]{2,1,0:T(4,128)(2,1)} %param.15) | copy-start | bytes 393220
  215.7 11.2 %collective-permute-start.11 = (f32[5,64,256]{2,1,0:T(8,128)S(1)}, f32[5,64,256]{2,1,0:T(8,128)S(1)}, u32[]{:S(2)}, u32[]{:S(2)}) collective-permute-start(f32[5,64,256]{2,1,0:T(8,128)S(1)} %get-tuple-element.35), channel_id=1, source_target_pairs={{0,8},{8,16},{16,24},{24,32},{32,40},{40,48},{48,56},{56,64},{64,7... | collective-permute-start | bytes 983048 | tf_op jit(solution)/shard_map/ppermute | solution.py:254
  223.0 10.5 %collective-permute-start.12 = (f32[5,64,256]{2,1,0:T(8,128)S(1)}, f32[5,64,256]{2,1,0:T(8,128)S(1)}, u32[]{:S(2)}, u32[]{:S(2)}) collective-permute-start(f32[5,64,256]{2,1,0:T(8,128)S(1)} %get-tuple-element.36), channel_id=1, source_target_pairs={{8,0},{16,8},{24,16},{32,24},{40,32},{48,40},{56,48},{64,56},{72,6... | collective-permute-start | bytes 983048 | tf_op jit(solution)/shard_map/ppermute | solution.py:255
where the time goes:
time: 237 us; the launch traced here: 236 us
  waiting for transfers between devices  131 us (55%)
  starting transfers between devices  87.7 us (37%)
  Pallas kernels  6.91 us (3%)
  local copies, waits for them, and re-layouts  4.99 us (2%)
  matrix products  4.14 us (2%)
    all_to_all x2, waiting for transfers between devices, transposed(): return lax.all_to_all(sent, chips, split_axis=0, concat_axis=0, tiled=True)  110 us
    all_to_all x2, starting transfers between devices, transposed(): return lax.all_to_all(sent, chips, split_axis=0, concat_axis=0, tiled=True)  31.6 us
    ppermute x7, starting transfers between devices, gather_ring(): lax.ppermute(block, axis, [(i, (i + hop) % count) for i in range(count)])  20.7 us
    ppermute x1, starting transfers between devices, inv_x_pair(): theirs = lax.ppermute(mine, 'zh', swap)  15.4 us
    ppermute x7, waiting for transfers between devices, gather_ring(): lax.ppermute(block, axis, [(i, (i + hop) % count) for i in range(count)])  12.1 us
    ppermute x2, starting transfers between devices, before_and_after(): before = lax.ppermute(tail, axes, [(i, i + 1) for i in range(count - 1)])  11.2 us
    ppermute x2, waiting for transfers between devices, before_and_after(): after = lax.ppermute(head, axes, [(i + 1, i) for i in range(count - 1)])  6.51 us
    ppermute x1, starting transfers between devices, body(): other = lax.ppermute(got, 'co', swap)  5.56 us
  transfers between devices with their start and end apart: 15, of which 8 were waited for; matrix products, arithmetic and copies ran while one was open for 3% of the time, Pallas kernels for 0%

commit v1 on v0

--- a/solution.py
+++ b/solution.py
@@ -52,31 +52,40 @@
     return pair.reshape(pair.shape[0], -1, pair.shape[-1])
 
 
-def pushes(marker_x, marker_z, marker_y, drag_weight, x_rows, z_rows, y_cells):
-    x_offset = lax.axis_index(grp) * x_rows
-    z_offset = lax.axis_index(slab) * z_rows
-    local_x = marker_x - x_offset
-    local_z = marker_z - z_offset
-    inside = (local_x >= 0) & (local_x < x_rows) & (local_z >= 0) & (local_z < z_rows)
-    cell = jnp.where(inside, local_x * z_rows + local_z, -1)
-    cells = lax.broadcasted_iota(jnp.int32, (x_rows * z_rows, 1), 0)
-    here = (cells == cell[None, :]).astype(jnp.float32)
-    lanes = lax.broadcasted_iota(jnp.int32, (1, y_cells), 1)
-    weighted = jnp.where(marker_y[:, None] == lanes, drag_weight[:, None], 0.0)
-    out = jnp.dot(here, weighted, precision=highest)
-    return out.reshape(x_rows, z_rows, y_cells)
+def z_of(k, which, half, z_rows):
+    groups = half // z_rows
+    return (k % groups) * (2 * z_rows) + which * z_rows + k // groups
+
+
+def push_plane(marker_x, marker_z, marker_y, drag_weight, inv_y, x_rows, z_rows):
+    y_cells = inv_y.shape[0]
+    core = lax.axis_index("co")
+    y_mine = lax.axis_index(chips)
+    to_y = lax.dynamic_slice_in_dim(inv_y, y_mine, 1, axis=1)
+    at_y = marker_y[:, None] == lax.broadcasted_iota(jnp.int32, (1, y_cells), 1)
+    amount = drag_weight * jnp.dot(at_y.astype(jnp.float32), to_y, precision=highest)[:, 0]
+    z_count = 2 * lax.axis_size("zl") * lax.axis_size("xx") * z_rows
+    row = lax.broadcasted_iota(jnp.int32, (z_count, 1), 0)
+    half = z_count // 2
+    z_row = jnp.where(row < half, z_of(row, core, half, z_rows), z_of(row - half, 1 - core, half, z_rows))
+    y_size, h_size = lax.axis_size("yy"), lax.axis_size("zh")
+    lane = lax.broadcasted_iota(jnp.int32, (1, y_size * h_size * x_rows), 1)
+    block = lane // x_rows
+    x_lane = ((block % h_size) * y_size + block // h_size) * x_rows + lane % x_rows
+    at_z = (z_row == marker_z[None, :]).astype(jnp.float32)
+    at_x = jnp.where(marker_x[:, None] == x_lane, amount[:, None], 0.0)
+    return jnp.dot(at_z, at_x, precision=highest)
 
 
 def z_weights(inv_z, z_rows):
     count = inv_z.shape[0]
     half = count // 2
-    groups = half // z_rows
     core = lax.axis_index("co")
 
     def chosen(which):
         k = lax.broadcasted_iota(jnp.int32, (half, count), 0)
         z = lax.broadcasted_iota(jnp.int32, (half, count), 1)
-        return (z == (k % groups) * (2 * z_rows) + which * z_rows + k // groups).astype(jnp.float32)
+        return (z == z_of(k, which, half, z_rows)).astype(jnp.float32)
 
     mine = chosen(core)
     both = jnp.concatenate([mine, chosen(1 - core)], axis=0)
@@ -84,7 +93,7 @@
     return jnp.einsum("bw,aw->ba", mine, picked, precision=highest)
 
 
-def solve_kernel(fields, own_ref, other_ref, wz_high, wz_low, ix_high, ix_low, out_ref, z_ref, edge_ref):
+def solve_kernel(fields, own_ref, other_ref, push_ref, wz_high, wz_low, ix_high, ix_low, out_ref, z_ref, edge_ref):
     rows = own_ref.shape[0] // 256
     out_rows = out_ref.shape[0] // 256
     lane = lax.broadcasted_iota(jnp.int32, (32, 128), 1)
@@ -107,6 +116,8 @@
     wz = wz_high[...], wz_low[...]
     for c in range(fields):
         both = jnp.concatenate([lines(own_ref, c), lines(other_ref, c)], axis=0)
+        if c == 0:
+            both = both + push_ref[...]
         z_ref[pl.ds(c * 128, 128), :] = product(wz, parts(both))
     ix = ix_high[...], ix_low[...]
     edge_ref[...] = jnp.zeros_like(edge_ref)
@@ -140,18 +151,47 @@
 params = pltpu.CompilerParams(vmem_limit_bytes=24 * 2**20)
 
 
-def solve_lines(own, other, weights, fields):
+def solve_lines(own, other, push, weights, fields):
     return pl.pallas_call(
         functools.partial(solve_kernel, fields),
         out_shape=jax.ShapeDtypeStruct((own.shape[0] + 256, 128), jnp.float32),
-        in_specs=[vmem] * 6,
+        in_specs=[vmem] * 7,
         out_specs=vmem,
         scratch_shapes=[pltpu.VMEM((fields * 128, 512), jnp.float32), pltpu.VMEM((8, 32, 128), jnp.float32)],
         compiler_params=params,
         cost_estimate=pl.CostEstimate(
             flops=fields * 128 * 512 * (512 + 256) * 6, bytes_accessed=8 * 2**20, transcendentals=0
         ),
-    )(own, other, *weights)
+    )(own, other, push, *weights)
+
+
+def y_kernel(fields, cells_ref, inv_ref, out_ref):
+    inv = parts(inv_ref[...].T)
+    rows = 2 * fields
+    contract = (((1,), (1,)), ((), ()))
+    dot = lambda a, b: lax.dot_general(a, b, contract, preferred_element_type=jnp.float32)
+    for c in range(fields):
+        for pair in range(2):
+            both = []
+            for z in (2 * pair, 2 * pair + 1):
+                tiles = [cells_ref[pl.ds(c * 512 + 4 * tile + z, 64, stride=8), :] for tile in range(2)]
+                both.append(jnp.concatenate(tiles, axis=1))
+            high, low = parts(jnp.concatenate(both, axis=0))
+            done = dot(inv[0], high) + (dot(inv[0], low) + dot(inv[1], high))
+            out_ref[pl.ds(2 * c + pair, 256, stride=rows), :] = done
+
+
+def y_solved(cells, inv_y):
+    fields, x_rows, z_rows, y_cells = cells.shape
+    tiles = cells.reshape(fields, x_rows, z_rows, y_cells // 128, 128).transpose(0, 1, 3, 2, 4).reshape(-1, 128)
+    return pl.pallas_call(
+        functools.partial(y_kernel, fields),
+        out_shape=jax.ShapeDtypeStruct(tiles.shape, jnp.float32),
+        in_specs=[vmem] * 2,
+        out_specs=vmem,
+        compiler_params=params,
+        cost_estimate=pl.CostEstimate(flops=6 * tiles.size * y_cells, bytes_accessed=3 * 2**20, transcendentals=0),
+    )(tiles, inv_y)
 
 
 def weights_kernel(wz_ref, ix_ref, wz_high, wz_low, ix_high, ix_low):
@@ -276,11 +316,9 @@
     fields, x_rows, z_rows, y_cells = adj_out.shape
     pair = inv_x_pair(inv_x)
     wz = z_weights(inv_z, z_rows)
-    pushed = pushes(marker_x, marker_z, marker_y, drag_weight, x_rows, z_rows, y_cells)
-    seeded = adj_out.at[0].add(pushed)
-    ysolved = jnp.einsum("lm,cxzl->mczx", inv_y, seeded, precision=highest)
-    pair, sent = lax.optimization_barrier((pair, ysolved.reshape(y_cells, fields * z_rows * x_rows)))
+    sent = y_solved(adj_out, inv_y).reshape(y_cells, -1)
     got = transposed(sent).reshape(-1, 128)
+    push = push_plane(marker_x, marker_z, marker_y, drag_weight, inv_y, x_rows, z_rows)
     full_x = whole_inv_x(pair)
     weights = prepared(wz, full_x)
     mask = body_mask.astype(jnp.float32).transpose(1, 0, 2)
@@ -288,7 +326,7 @@
     flow = advect.astype(jnp.float32).transpose(0, 2, 1, 3)
     thick = viscosity.astype(jnp.float32).transpose(1, 0, 2)
     other = lax.ppermute(got, "co", swap)
-    back = solve_lines(got, other, weights, fields)
+    back = solve_lines(got, other, push, weights, fields)
     solved = transposed(back.reshape(y_cells, -1)).reshape(-1, 128)
     masked, low, high, edges = masked_cells(solved, mask, fields)
     below, above = before_and_after(low, high, slab)

time: 237 us -> 240 us (1.013)
  waiting for transfers between devices: 131 us -> 120 us
  starting transfers between devices: 87.7 us -> 93.5 us
  local copies, waits for them, and re-layouts: 4.99 us -> 8.69 us
    all_to_all x2, waiting for transfers between devices: 110 us -> 63.7 us  [transposed(): return lax.all_to_all(sent, chips, split_axis=0, concat_axis=0, tiled=True)]
    ppermute x1, waiting for transfers between devices: 0.01 us -> 40.7 us  [inv_x_pair(): theirs = lax.ppermute(mine, 'zh', swap)]
    all_to_all x2, starting transfers between devices: 31.6 us -> 39.3 us  [transposed(): return lax.all_to_all(sent, chips, split_axis=0, concat_axis=0, tiled=True)]
    ppermute x7, starting transfers between devices: 20.7 us -> 25.1 us  [gather_ring(): lax.ppermute(block, axis, [(i, (i + hop) % count) for i in range(count)])]
    ppermute x7, waiting for transfers between devices: 12.1 us -> 8.11 us  [gather_ring(): lax.ppermute(block, axis, [(i, (i + hop) % count) for i in range(count)])]
    ppermute x1, starting transfers between devices: 15.4 us -> 11.8 us  [inv_x_pair(): theirs = lax.ppermute(mine, 'zh', swap)]
    ppermute x1, starting transfers between devices: 5.56 us -> 2.81 us  [body(): other = lax.ppermute(got, 'co', swap)]
  transfers between devices with their start and end apart: 15 -> 15, of which waited for: 8 -> 7; matrix products, arithmetic and copies ran while one was open for 3% -> 5% of each run, Pallas kernels for 0% -> 0%
where the time goes in v1:
time: 240 us
  waiting for transfers between devices  120 us (50%)
  starting transfers between devices  93.5 us (39%)
  Pallas kernels  9.3 us (4%)
  local copies, waits for them, and re-layouts  8.69 us (4%)
  matrix products  5.96 us (2%)
    all_to_all x2, waiting for transfers between devices, transposed(): return lax.all_to_all(sent, chips, split_axis=0, concat_axis=0, tiled=True)  63.7 us
    ppermute x1, waiting for transfers between devices, inv_x_pair(): theirs = lax.ppermute(mine, 'zh', swap)  40.7 us
    all_to_all x2, starting transfers between devices, transposed(): return lax.all_to_all(sent, chips, split_axis=0, concat_axis=0, tiled=True)  39.3 us
    ppermute x7, starting transfers between devices, gather_ring(): lax.ppermute(block, axis, [(i, (i + hop) % count) for i in range(count)])  25.1 us
    ppermute x1, starting transfers between devices, inv_x_pair(): theirs = lax.ppermute(mine, 'zh', swap)  11.8 us
    ppermute x2, starting transfers between devices, before_and_after(): before = lax.ppermute(tail, axes, [(i, i + 1) for i in range(count - 1)])  11.2 us
    ppermute x7, waiting for transfers between devices, gather_ring(): lax.ppermute(block, axis, [(i, (i + hop) % count) for i in range(count)])  8.11 us
    ppermute x2, waiting for transfers between devices, before_and_after(): after = lax.ppermute(head, axes, [(i + 1, i) for i in range(count - 1)])  6.51 us
  transfers between devices with their start and end apart: 15, of which 7 were waited for; matrix products, arithmetic and copies ran while one was open for 5% of the time, Pallas kernels for 0%

profile of v1, /device:TPU:7, one launch (start us, length us, event | category | flops | bytes accessed | tf_op | source)
XLA Modules:
  0.0 239.5 jit_solution(11120760702248096754)
XLA Ops:
  0.0 1.4 copy-done.1
  1.4 0.9 copy-done.2
  2.3 2.3 shard_map.109
  4.7 23.1 %all-to-all-start = ((f32[256,1,1280]{2,1,0:T(1,128)}), f32[256,1,1280]{2,1,0:T(1,128)S(1)}, u32[]{:S(2)}, u32[]{:S(2)}) async-start(f32[256,1,1280]{2,1,0:T(1,128)} %bitcast.3), calls=%async_computation | async-start | bytes 2621440 | tf_op jit(solution)/shard_map/all_to_all | solution.py:300
  27.9 11.8 %collective-permute-start.1 = (f32[64,64]{0,1:T(8,128)S(1)}, f32[64,64]{0,1:T(8,128)S(1)}, u32[]{:S(2)}, u32[]{:S(2)}) collective-permute-start(f32[64,64]{0,1:T(8,128)S(1)} %constant_dynamic-slice_fusion), channel_id=1, source_target_pairs={{0,4},{4,0},{1,5},{5,1},{2,6},{6,2},{3,7},{7,3},{8,12},{12,8},{9,1... | collective-permute-start | bytes 49160 | tf_op jit(solution)/shard_map/ppermute | solution.py:44
  40.0 1.0 fusion.8
  41.8 2.6 %fusion.push_ref = f32[256,512]{1,0:T(8,128)S(1)} fusion(f32[2048]{0:T(1024)S(1)} %mul.78, s32[512]{0:T(512)S(1)} %fusion.25, s32[2048]{0:T(1024)S(1)} %copy-done.11, s32[2048]{0:T(1024)S(1)} %copy-done.12, s32[256]{0:T(256)S(1)} %compare_select_fusion), kind=kOutput, calls=%fused_computation | convolution fusion | flops 3223846912 | bytes 551936 | tf_op jit(solution)/shard_map/dot_general | solution.py:77
  44.5 1.0 fusion.12
  45.5 40.7 %collective-permute-done.1 = f32[64,64]{0,1:T(8,128)S(1)} collective-permute-done((f32[64,64]{0,1:T(8,128)S(1)}, f32[64,64]{0,1:T(8,128)S(1)}, u32[]{:S(2)}, u32[]{:S(2)}) %collective-permute-start.1) | collective-permute-done | bytes 16416 | tf_op jit(solution)/shard_map/ppermute | solution.py:44
  86.4 7.1 %collective-permute-start.2 = (f32[64,128]{0,1:T(8,128)S(1)}, f32[64,128]{0,1:T(8,128)S(1)}, u32[]{:S(2)}, u32[]{:S(2)}) collective-permute-start(f32[64,128]{0,1:T(8,128)S(1)} %get-tuple-element.23), channel_id=1, source_target_pairs={{0,8},{8,0},{1,9},{9,1},{2,10},{10,2},{3,11},{11,3},{4,12},{12,4},... | collective-permute-start | bytes 98312 | tf_op jit(solution)/shard_map/ppermute | solution.py:35
  94.5 3.1 %collective-permute-start.3 = (f32[2,64,128]{2,1,0:T(8,128)S(1)}, f32[2,64,128]{2,1,0:T(8,128)S(1)}, u32[]{:S(2)}, u32[]{:S(2)}) collective-permute-start(f32[2,64,128]{2,1,0:T(8,128)S(1)} %constant_dynamic-update-slice_fusion), channel_id=1, source_target_pairs={{0,16},{16,32},{32,48},{48,0},{1,17},{17,33},{33,49},{49,1},{2,18}... | collective-permute-start | bytes 196616 | tf_op jit(solution)/shard_map/ppermute | solution.py:35
  97.6 3.5 %collective-permute-start.4 = (f32[2,64,128]{2,1,0:T(8,128)S(1)}, f32[2,64,128]{2,1,0:T(8,128)S(1)}, u32[]{:S(2)}, u32[]{:S(2)}) collective-permute-start(f32[2,64,128]{2,1,0:T(8,128)S(1)} %constant_dynamic-update-slice_fusion), channel_id=1, source_target_pairs={{0,32},{16,48},{32,0},{48,16},{1,33},{17,49},{33,1},{49,17},{2,34}... | collective-permute-start | bytes 196616 | tf_op jit(solution)/shard_map/ppermute | solution.py:35
  101.2 1.9 collective-permute-start.5
  105.7 2.8 %collective-permute-start = (f32[2560,128]{1,0:T(8,128)S(1)}, f32[2560,128]{1,0:T(8,128)S(1)}, u32[]{:S(2)}, u32[]{:S(2)}) collective-permute-start(f32[2560,128]{1,0:T(8,128)S(1)} %bitcast.50), channel_id=1, source_target_pairs={{0,8},{8,0},{1,9},{9,1},{2,10},{10,2},{3,11},{11,3},{4,12},{12,4},... | collective-permute-start | bytes 3932168 | tf_op jit(solution)/shard_map/ppermute | solution.py:328
  109.2 1.9 collective-permute-start.6
  111.1 1.3 fusion.43.wz_ref
  112.5 5.3 %collective-permute-start.7 = (f32[4,2,64,128]{3,2,1,0:T(8,128)}, f32[4,2,64,128]{3,2,1,0:T(8,128)S(1)}, u32[]{:S(2)}, u32[]{:S(2)}) collective-permute-start(f32[4,2,64,128]{3,2,1,0:T(8,128)} %bitcast_dynamic-update-slice_fusion.4), channel_id=1, source_target_pairs={{0,2},{1,3},{2,0},{3,1},{4,6},{5,7},{6,4},{7,5},{8,10},{9,11},{10,... | collective-permute-start | bytes 786440 | tf_op jit(solution)/shard_map/ppermute | solution.py:35
  117.8 2.1 collective-permute-start.8
  120.0 1.0 bitcast_dynamic-update-slice_fusion.3
  121.0 1.0 bitcast_dynamic-update-slice_fusion.2
  122.0 4.3 %collective-permute-done.7 = f32[4,2,64,128]{3,2,1,0:T(8,128)S(1)} collective-permute-done((f32[4,2,64,128]{3,2,1,0:T(8,128)}, f32[4,2,64,128]{3,2,1,0:T(8,128)S(1)}, u32[]{:S(2)}, u32[]{:S(2)}) %collective-permute-start.7) | collective-permute-done | bytes 262176 | tf_op jit(solution)/shard_map/ppermute | solution.py:35
  126.3 3.0 %collective-permute-done.8 = f32[4,2,64,128]{3,2,1,0:T(8,128)S(1)} collective-permute-done((f32[4,2,64,128]{3,2,1,0:T(8,128)}, f32[4,2,64,128]{3,2,1,0:T(8,128)S(1)}, u32[]{:S(2)}, u32[]{:S(2)}) %collective-permute-start.8) | collective-permute-done | bytes 262176 | tf_op jit(solution)/shard_map/ppermute | solution.py:35
  129.5 4.0 %shard_map.111 = f32[2816,128]{1,0:T(8,128)} custom-call(f32[2560,128]{1,0:T(8,128)S(1)} %bitcast.51, f32[2560,128]{1,0:T(8,128)S(1)} %collective-permute-done.other_ref, f32[256,512]{1,0:T(8,128)S(1)} %fusion.push_ref, bf16[128,256]{1,0:T(8,128)(2,1)S(1)} %get-tuple-element.13.wz_high, bf16[128,256]{1,0:T(8,128)(2,1)S(1)} %get-tuple-element.14.wz_low, ...), custom_call_target="tpu_custom_call" | custom-call | flops 1509949440 | bytes 8388608 | tf_op jit(solution)/shard_map/pallas_call | solution.py:155
  133.5 16.2 %all-to-all-start.1 = ((f32[256,1,1408]{2,1,0:T(1,128)}), f32[256,1,1408]{2,1,0:T(1,128)S(1)}, u32[]{:S(2)}, u32[]{:S(2)}) async-start(f32[256,1,1408]{2,1,0:T(1,128)} %bitcast.17), calls=%async_computation.1 | async-start | bytes 2883584 | tf_op jit(solution)/shard_map/all_to_all | solution.py:300
  149.8 1.3 collective-permute-start.10
  151.1 4.0 %collective-permute-start.9 = (f32[4,256]{1,0:T(4,128)S(1)}, f32[4,256]{1,0:T(4,128)S(1)}, u32[]{:S(2)}, u32[]{:S(2)}) collective-permute-start(f32[4,256]{1,0:T(4,128)S(1)} %get-tuple-element.21), channel_id=1, source_target_pairs={{0,1},{1,2},{2,3},{3,4},{4,5},{5,6},{6,7},{8,9},{9,10},{10,11},{11... | collective-permute-start | bytes 12296 | tf_op jit(solution)/shard_map/ppermute | solution.py:294
  155.2 63.7 %all-to-all-done.1 = f32[256,1,1408]{2,1,0:T(1,128)S(1)} async-done(((f32[256,1,1408]{2,1,0:T(1,128)}), f32[256,1,1408]{2,1,0:T(1,128)S(1)}, u32[]{:S(2)}, u32[]{:S(2)}) %all-to-all-start.1) | async-done | bytes 1441824 | tf_op jit(solution)/shard_map/all_to_all | solution.py:300
  219.4 7.2 %collective-permute-start.11 = (f32[5,64,256]{2,1,0:T(8,128)S(1)}, f32[5,64,256]{2,1,0:T(8,128)S(1)}, u32[]{:S(2)}, u32[]{:S(2)}) collective-permute-start(f32[5,64,256]{2,1,0:T(8,128)S(1)} %get-tuple-element.19), channel_id=1, source_target_pairs={{0,8},{8,16},{16,24},{24,32},{32,40},{40,48},{48,56},{56,64},{64,7... | collective-permute-start | bytes 983048 | tf_op jit(solution)/shard_map/ppermute | solution.py:294
  226.6 1.9 collective-permute-start.12
  229.5 1.1 collective-permute-done.11.below_ref
  230.6 6.5 %collective-permute-done.12.above_ref = f32[5,64,256]{2,1,0:T(8,128)S(1)} collective-permute-done((f32[5,64,256]{2,1,0:T(8,128)S(1)}, f32[5,64,256]{2,1,0:T(8,128)S(1)}, u32[]{:S(2)}, u32[]{:S(2)}) %collective-permute-start.12) | collective-permute-done | bytes 327712 | tf_op jit(solution)/shard_map/ppermute | solution.py:295
  237.1 2.4 %shard_map.113 = f32[2560,128]{1,0:T(8,128)} custom-call(f32[5,4,64,256]{3,2,1,0:T(8,128)S(1)} %get-tuple-element.17.masked_ref, f32[40,256]{1,0:T(8,128)S(1)} %get-tuple-element.18.edge_ref, f32[8,256]{1,0:T(8,128)S(1)} %pad_maximum_fusion.1.rim_ref, f32[5,64,256]{2,1,0:T(8,128)S(1)} %collective-permute-done.11.below_ref, ...), custom_call_target="tpu_custom_call" | custom-call | flops 8388608 | bytes 5242880 | tf_op jit(solution)/shard_map/pallas_call | solution.py:280
  (65 shorter events, 7.2 us)
Async XLA Ops:
  0.0 44.5 %copy-start = (f32[256,256]{1,0:T(8,128)S(1)}, f32[256,256]{1,0:T(8,128)}, u32[]{:S(2)}) copy-start(f32[256,256]{1,0:T(8,128)} %param.21) | copy-start | bytes 786436
  0.0 1.4 copy-start.1
  1.4 0.9 copy-start.2
  4.6 23.2 %copy-start.6 = (f32[512,64]{0,1:T(8,128)S(1)}, f32[512,64]{0,1:T(8,128)}, u32[]{:S(2)}) copy-start(f32[512,64]{0,1:T(8,128)} %param.19) | copy-start | bytes 393220
  4.6 35.1 %copy-start.3 = (f32[256,256]{1,0:T(8,128)S(1)}, f32[256,256]{1,0:T(8,128)}, u32[]{:S(2)}) copy-start(f32[256,256]{1,0:T(8,128)} %inv_ref.1) | copy-start | bytes 786436
  4.6 35.3 %copy-start.10 = (s32[2048]{0:T(1024)S(1)}, s32[2048]{0:T(1024)}, u32[]{:S(2)}) copy-start(s32[2048]{0:T(1024)} %param.17) | copy-start | bytes 24580
  4.6 36.4 %copy-start.7 = (f32[2048]{0:T(1024)S(1)}, f32[2048]{0:T(1024)}, u32[]{:S(2)}) copy-start(f32[2048]{0:T(1024)} %param.18) | copy-start | bytes 24580
  4.6 37.2 %copy-start.11 = (s32[2048]{0:T(1024)S(1)}, s32[2048]{0:T(1024)}, u32[]{:S(2)}) copy-start(s32[2048]{0:T(1024)} %param.15) | copy-start | bytes 24580
  4.6 37.2 %copy-start.12 = (s32[2048]{0:T(1024)S(1)}, s32[2048]{0:T(1024)}, u32[]{:S(2)}) copy-start(s32[2048]{0:T(1024)} %param.16) | copy-start | bytes 24580
  4.7 101.1 %all-to-all-start = ((f32[256,1,1280]{2,1,0:T(1,128)}), f32[256,1,1280]{2,1,0:T(1,128)S(1)}, u32[]{:S(2)}, u32[]{:S(2)}) async-start(f32[256,1,1280]{2,1,0:T(1,128)} %bitcast.3), calls=%async_computation | async-start | bytes 2621440 | tf_op jit(solution)/shard_map/all_to_all | solution.py:300
  27.9 58.3 %collective-permute-start.1 = (f32[64,64]{0,1:T(8,128)S(1)}, f32[64,64]{0,1:T(8,128)S(1)}, u32[]{:S(2)}, u32[]{:S(2)}) collective-permute-start(f32[64,64]{0,1:T(8,128)S(1)} %constant_dynamic-slice_fusion), channel_id=1, source_target_pairs={{0,4},{4,0},{1,5},{5,1},{2,6},{6,2},{3,7},{7,3},{8,12},{12,8},{9,1... | collective-permute-start | bytes 49160 | tf_op jit(solution)/shard_map/ppermute | solution.py:44
  41.1 0.6 copy-start.8
  41.1 0.6 copy-start.9
  86.4 8.0 %collective-permute-start.2 = (f32[64,128]{0,1:T(8,128)S(1)}, f32[64,128]{0,1:T(8,128)S(1)}, u32[]{:S(2)}, u32[]{:S(2)}) collective-permute-start(f32[64,128]{0,1:T(8,128)S(1)} %get-tuple-element.23), channel_id=1, source_target_pairs={{0,8},{8,0},{1,9},{9,1},{2,10},{10,2},{3,11},{11,3},{4,12},{12,4},... | collective-permute-start | bytes 98312 | tf_op jit(solution)/shard_map/ppermute | solution.py:35
  94.5 10.0 %collective-permute-start.3 = (f32[2,64,128]{2,1,0:T(8,128)S(1)}, f32[2,64,128]{2,1,0:T(8,128)S(1)}, u32[]{:S(2)}, u32[]{:S(2)}) collective-permute-start(f32[2,64,128]{2,1,0:T(8,128)S(1)} %constant_dynamic-update-slice_fusion), channel_id=1, source_target_pairs={{0,16},{16,32},{32,48},{48,0},{1,17},{17,33},{33,49},{49,1},{2,18}... | collective-permute-start | bytes 196616 | tf_op jit(solution)/shard_map/ppermute | solution.py:35
  97.6 7.5 %collective-permute-start.4 = (f32[2,64,128]{2,1,0:T(8,128)S(1)}, f32[2,64,128]{2,1,0:T(8,128)S(1)}, u32[]{:S(2)}, u32[]{:S(2)}) collective-permute-start(f32[2,64,128]{2,1,0:T(8,128)S(1)} %constant_dynamic-update-slice_fusion), channel_id=1, source_target_pairs={{0,32},{16,48},{32,0},{48,16},{1,33},{17,49},{33,1},{49,17},{2,34}... | collective-permute-start | bytes 196616 | tf_op jit(solution)/shard_map/ppermute | solution.py:35
  101.2 7.4 %collective-permute-start.5 = (f32[2,64,128]{2,1,0:T(8,128)S(1)}, f32[2,64,128]{2,1,0:T(8,128)S(1)}, u32[]{:S(2)}, u32[]{:S(2)}) collective-permute-start(f32[2,64,128]{2,1,0:T(8,128)S(1)} %constant_dynamic-update-slice_fusion), channel_id=1, source_target_pairs={{0,48},{16,0},{32,16},{48,32},{1,49},{17,1},{33,17},{49,33},{2,50}... | collective-permute-start | bytes 196616 | tf_op jit(solution)/shard_map/ppermute | solution.py:35
  105.7 23.7 %collective-permute-start = (f32[2560,128]{1,0:T(8,128)S(1)}, f32[2560,128]{1,0:T(8,128)S(1)}, u32[]{:S(2)}, u32[]{:S(2)}) collective-permute-start(f32[2560,128]{1,0:T(8,128)S(1)} %bitcast.50), channel_id=1, source_target_pairs={{0,8},{8,0},{1,9},{9,1},{2,10},{10,2},{3,11},{11,3},{4,12},{12,4},... | collective-permute-start | bytes 3932168 | tf_op jit(solution)/shard_map/ppermute | solution.py:328
  109.2 11.8 %collective-permute-start.6 = (f32[4,2,64,128]{3,2,1,0:T(8,128)}, f32[4,2,64,128]{3,2,1,0:T(8,128)}, u32[]{:S(2)}, u32[]{:S(2)}) collective-permute-start(f32[4,2,64,128]{3,2,1,0:T(8,128)} %bitcast_dynamic-update-slice_fusion.4), channel_id=1, source_target_pairs={{0,1},{1,2},{2,3},{3,0},{4,5},{5,6},{6,7},{7,4},{8,9},{9,10},{10,1... | collective-permute-start | bytes 786440 | tf_op jit(solution)/shard_map/ppermute | solution.py:35
  112.5 13.8 %collective-permute-start.7 = (f32[4,2,64,128]{3,2,1,0:T(8,128)}, f32[4,2,64,128]{3,2,1,0:T(8,128)S(1)}, u32[]{:S(2)}, u32[]{:S(2)}) collective-permute-start(f32[4,2,64,128]{3,2,1,0:T(8,128)} %bitcast_dynamic-update-slice_fusion.4), channel_id=1, source_target_pairs={{0,2},{1,3},{2,0},{3,1},{4,6},{5,7},{6,4},{7,5},{8,10},{9,11},{10,... | collective-permute-start | bytes 786440 | tf_op jit(solution)/shard_map/ppermute | solution.py:35
  117.8 11.5 %collective-permute-start.8 = (f32[4,2,64,128]{3,2,1,0:T(8,128)}, f32[4,2,64,128]{3,2,1,0:T(8,128)S(1)}, u32[]{:S(2)}, u32[]{:S(2)}) collective-permute-start(f32[4,2,64,128]{3,2,1,0:T(8,128)} %bitcast_dynamic-update-slice_fusion.4), channel_id=1, source_target_pairs={{0,3},{1,0},{2,1},{3,2},{4,7},{5,4},{6,5},{7,6},{8,11},{9,8},{10,9... | collective-permute-start | bytes 786440 | tf_op jit(solution)/shard_map/ppermute | solution.py:35
  133.5 16.2 %copy-start.5 = (s32[64,4,256]{2,1,0:T(4,128)S(1)}, s32[64,4,256]{2,1,0:T(4,128)}, u32[]{:S(2)}) copy-start(s32[64,4,256]{2,1,0:T(4,128)} %param.14) | copy-start | bytes 786436
  133.5 21.7 %copy-start.4 = (bf16[3,64,4,256]{3,2,1,0:T(4,128)(2,1)S(1)}, bf16[3,64,4,256]{3,2,1,0:T(4,128)(2,1)}, u32[]{:S(2)}) copy-start(bf16[3,64,4,256]{3,2,1,0:T(4,128)(2,1)} %param.12) | copy-start | bytes 1179652
  133.5 85.5 %all-to-all-start.1 = ((f32[256,1,1408]{2,1,0:T(1,128)}), f32[256,1,1408]{2,1,0:T(1,128)S(1)}, u32[]{:S(2)}, u32[]{:S(2)}) async-start(f32[256,1,1408]{2,1,0:T(1,128)} %bitcast.17), calls=%async_computation.1 | async-start | bytes 2883584 | tf_op jit(solution)/shard_map/all_to_all | solution.py:300
  149.8 79.7 %collective-permute-start.10 = (f32[4,256]{1,0:T(4,128)S(1)}, f32[4,256]{1,0:T(4,128)S(1)}, u32[]{:S(2)}, u32[]{:S(2)}) collective-permute-start(f32[4,256]{1,0:T(4,128)S(1)} %get-tuple-element.22), channel_id=1, source_target_pairs={{1,0},{2,1},{3,2},{4,3},{5,4},{6,5},{7,6},{9,8},{10,9},{11,10},{12... | collective-permute-start | bytes 12296 | tf_op jit(solution)/shard_map/ppermute | solution.py:295
  151.1 78.4 %collective-permute-start.9 = (f32[4,256]{1,0:T(4,128)S(1)}, f32[4,256]{1,0:T(4,128)S(1)}, u32[]{:S(2)}, u32[]{:S(2)}) collective-permute-start(f32[4,256]{1,0:T(4,128)S(1)} %get-tuple-element.21), channel_id=1, source_target_pairs={{0,1},{1,2},{2,3},{3,4},{4,5},{5,6},{6,7},{8,9},{9,10},{10,11},{11... | collective-permute-start | bytes 12296 | tf_op jit(solution)/shard_map/ppermute | solution.py:294
  219.4 11.2 %collective-permute-start.11 = (f32[5,64,256]{2,1,0:T(8,128)S(1)}, f32[5,64,256]{2,1,0:T(8,128)S(1)}, u32[]{:S(2)}, u32[]{:S(2)}) collective-permute-start(f32[5,64,256]{2,1,0:T(8,128)S(1)} %get-tuple-element.19), channel_id=1, source_target_pairs={{0,8},{8,16},{16,24},{24,32},{32,40},{40,48},{48,56},{56,64},{64,7... | collective-permute-start | bytes 983048 | tf_op jit(solution)/shard_map/ppermute | solution.py:294
  226.6 10.5 %collective-permute-start.12 = (f32[5,64,256]{2,1,0:T(8,128)S(1)}, f32[5,64,256]{2,1,0:T(8,128)S(1)}, u32[]{:S(2)}, u32[]{:S(2)}) collective-permute-start(f32[5,64,256]{2,1,0:T(8,128)S(1)} %get-tuple-element.20), channel_id=1, source_target_pairs={{8,0},{16,8},{24,16},{32,24},{40,32},{48,40},{56,48},{64,56},{72,6... | collective-permute-start | bytes 983048 | tf_op jit(solution)/shard_map/ppermute | solution.py:295

commit v2 on v1

--- a/solution.py
+++ b/solution.py
@@ -165,20 +165,23 @@
     )(own, other, push, *weights)
 
 
-def y_kernel(fields, cells_ref, inv_ref, out_ref):
-    inv = parts(inv_ref[...].T)
-    rows = 2 * fields
+def y_kernel(fields, cells_ref, inv_ref, out_ref, high_ref, low_ref):
+    c = pl.program_id(0)
+
+    @pl.when(c == 0)
+    def _():
+        high_ref[...], low_ref[...] = parts(inv_ref[...].T)
+
     contract = (((1,), (1,)), ((), ()))
     dot = lambda a, b: lax.dot_general(a, b, contract, preferred_element_type=jnp.float32)
-    for c in range(fields):
-        for pair in range(2):
-            both = []
-            for z in (2 * pair, 2 * pair + 1):
-                tiles = [cells_ref[pl.ds(c * 512 + 4 * tile + z, 64, stride=8), :] for tile in range(2)]
-                both.append(jnp.concatenate(tiles, axis=1))
-            high, low = parts(jnp.concatenate(both, axis=0))
-            done = dot(inv[0], high) + (dot(inv[0], low) + dot(inv[1], high))
-            out_ref[pl.ds(2 * c + pair, 256, stride=rows), :] = done
+    for pair in range(2):
+        both = []
+        for z in (2 * pair, 2 * pair + 1):
+            tiles = [cells_ref[pl.ds(4 * tile + z, 64, stride=8), :] for tile in range(2)]
+            both.append(jnp.concatenate(tiles, axis=1))
+        high, low = parts(jnp.concatenate(both, axis=0))
+        done = dot(high_ref[...], high) + (dot(high_ref[...], low) + dot(low_ref[...], high))
+        out_ref[pl.ds(2 * c + pair, 256, stride=2 * fields), :] = done
 
 
 def y_solved(cells, inv_y):
@@ -186,10 +189,15 @@
     tiles = cells.reshape(fields, x_rows, z_rows, y_cells // 128, 128).transpose(0, 1, 3, 2, 4).reshape(-1, 128)
     return pl.pallas_call(
         functools.partial(y_kernel, fields),
+        grid=(fields,),
         out_shape=jax.ShapeDtypeStruct(tiles.shape, jnp.float32),
-        in_specs=[vmem] * 2,
-        out_specs=vmem,
-        compiler_params=params,
+        in_specs=[
+            pl.BlockSpec((tiles.shape[0] // fields, 128), lambda c: (c, 0)),
+            pl.BlockSpec(inv_y.shape, lambda c: (0, 0)),
+        ],
+        out_specs=pl.BlockSpec(tiles.shape, lambda c: (0, 0)),
+        scratch_shapes=[pltpu.VMEM(inv_y.shape, jnp.bfloat16)] * 2,
+        compiler_params=pltpu.CompilerParams(vmem_limit_bytes=61000 * 1024),
         cost_estimate=pl.CostEstimate(flops=6 * tiles.size * y_cells, bytes_accessed=3 * 2**20, transcendentals=0),
     )(tiles, inv_y)
 
@@ -251,7 +259,7 @@
     )(got, mask)
 
 
-def stencil_kernel(fields, masked_ref, edge_ref, rim_ref, below_ref, above_ref, flow_ref, thick_ref, out_ref):
+def stencil_kernel(fields, masked_ref, edge_ref, rim_ref, flow_ref, thick_ref, out_ref):
     row = lax.broadcasted_iota(jnp.int32, (64, 256), 0)
     lane = lax.broadcasted_iota(jnp.int32, (64, 256), 1)
     for z in range(4):
@@ -266,25 +274,48 @@
             x_more = jnp.where(row == 63, last, pltpu.roll(v, 63, 0))
             y_less = jnp.where(lane == 0, 0.0, pltpu.roll(v, 1, 1))
             y_more = jnp.where(lane == 255, 0.0, pltpu.roll(v, 255, 1))
-            z_less = below_ref[c] if z == 0 else masked_ref[c, z - 1]
-            z_more = above_ref[c] if z == 3 else masked_ref[c, z + 1]
-            laplace = x_more + x_less + z_more + z_less + y_more + y_less - 6.0 * v
-            slopes = flow_x * (x_more - x_less) + flow_z * (z_more - z_less) + flow_y * (y_more - y_less)
-            done = v + time_step * (0.5 * slopes + thick * laplace)
+            around = x_more + x_less + y_more + y_less - 6.0 * v
+            slopes = flow_x * (x_more - x_less) + flow_y * (y_more - y_less)
+            if z > 0:
+                around, slopes = around + masked_ref[c, z - 1], slopes - flow_z * masked_ref[c, z - 1]
+            if z < 3:
+                around, slopes = around + masked_ref[c, z + 1], slopes + flow_z * masked_ref[c, z + 1]
+            done = v + time_step * (0.5 * slopes + thick * around)
             for half in range(2):
                 out_ref[pl.ds(c * 512 + half * 4 + z, 64, stride=8), :] = done[:, half * 128 : half * 128 + 128]
 
 
+def rim_kernel(fields, most_ref, below_ref, above_ref, flow_ref, thick_ref, out_ref):
+    low = time_step * (thick_ref[0] - 0.5 * flow_ref[1, 0])
+    high = time_step * (thick_ref[3] + 0.5 * flow_ref[1, 3])
+    for c in range(fields):
+        for z in range(4):
+            added = low * below_ref[c] if z == 0 else high * above_ref[c] if z == 3 else None
+            for half in range(2):
+                at = pl.ds(c * 512 + half * 4 + z, 64, stride=8)
+                value = most_ref[at, :]
+                out_ref[at, :] = value if added is None else value + added[:, half * 128 : half * 128 + 128]
+
+
 def stencil(masked, edges, rim, below, above, flow, thick):
     fields, z_rows, x_rows, y_cells = masked.shape
+    shape = jax.ShapeDtypeStruct((masked.size // 128, 128), jnp.float32)
+    most = pl.pallas_call(
+        functools.partial(stencil_kernel, fields),
+        out_shape=shape,
+        in_specs=[vmem] * 5,
+        out_specs=vmem,
+        compiler_params=params,
+        cost_estimate=pl.CostEstimate(flops=2**23, bytes_accessed=5 * 2**20, transcendentals=0),
+    )(masked, edges, rim, flow, thick)
     out = pl.pallas_call(
-        functools.partial(stencil_kernel, fields),
-        out_shape=jax.ShapeDtypeStruct((fields * x_rows * z_rows * y_cells // 128, 128), jnp.float32),
-        in_specs=[vmem] * 7,
+        functools.partial(rim_kernel, fields),
+        out_shape=shape,
+        in_specs=[vmem] * 5,
         out_specs=vmem,
         compiler_params=params,
-        cost_estimate=pl.CostEstimate(flops=2**23, bytes_accessed=5 * 2**20, transcendentals=0),
-    )(masked, edges, rim, below, above, flow, thick)
+        cost_estimate=pl.CostEstimate(flops=2**20, bytes_accessed=3 * 2**20, transcendentals=0),
+    )(most, below, above, flow, thick)
     out = out.reshape(fields, x_rows, y_cells // 128, z_rows, 128)
     return out.transpose(0, 1, 3, 2, 4).reshape(fields, x_rows, z_rows, y_cells)
 

time: 240 us -> 240 us (level)
    pallas_call x2 -> x3, Pallas kernels: 4.71 us -> 8.1 us  [the longest x1 5.33 us: y_solved(): pl.pallas_call(functools.partial(y_kernel, fields), grid=(fields,), out_s...]
  transfers between devices with their start and end apart: 15 -> 15, of which waited for: 7 -> 6; matrix products, arithmetic and copies ran while one was open for 5% -> 5% of each run, Pallas kernels for 0% -> 1%
where the time goes in v2:
time: 240 us; the launch traced here: 239 us
  waiting for transfers between devices  119 us (50%)
  starting transfers between devices  93.4 us (39%)
  Pallas kernels  11.5 us (5%)
  local copies, waits for them, and re-layouts  7.49 us (3%)
  matrix products  5.95 us (2%)
    all_to_all x2, waiting for transfers between devices, transposed(): return lax.all_to_all(sent, chips, split_axis=0, concat_axis=0, tiled=True)  63.7 us
    ppermute x1, waiting for transfers between devices, inv_x_pair(): theirs = lax.ppermute(mine, 'zh', swap)  40.7 us
    all_to_all x2, starting transfers between devices, transposed(): return lax.all_to_all(sent, chips, split_axis=0, concat_axis=0, tiled=True)  39.3 us
    ppermute x7, starting transfers between devices, gather_ring(): lax.ppermute(block, axis, [(i, (i + hop) % count) for i in range(count)])  25.1 us
    ppermute x1, starting transfers between devices, inv_x_pair(): theirs = lax.ppermute(mine, 'zh', swap)  11.8 us
    ppermute x2, starting transfers between devices, before_and_after(): before = lax.ppermute(tail, axes, [(i, i + 1) for i in range(count - 1)])  11.2 us
    ppermute x7, waiting for transfers between devices, gather_ring(): lax.ppermute(block, axis, [(i, (i + hop) % count) for i in range(count)])  8.1 us
    ppermute x2, waiting for transfers between devices, before_and_after(): after = lax.ppermute(head, axes, [(i + 1, i) for i in range(count - 1)])  6.28 us
  transfers between devices with their start and end apart: 15, of which 6 were waited for; matrix products, arithmetic and copies ran while one was open for 5% of the time, Pallas kernels for 1%

profile of v2, /device:TPU:7, one launch (start us, length us, event | category | flops | bytes accessed | tf_op | source)
XLA Modules:
  0.0 239.2 jit_solution(15481657507422944051)
XLA Ops:
  0.0 5.3 %shard_map.109 = f32[2560,128]{1,0:T(8,128)} custom-call(f32[2560,128]{1,0:T(8,128)} %bitcast.55, f32[256,256]{1,0:T(8,128)} %inv_ref.1), custom_call_target="tpu_custom_call" | custom-call | flops 503316480 | bytes 3145728 | tf_op jit(solution)/shard_map/pallas_call | solution.py:190
  5.4 23.1 %all-to-all-start = ((f32[256,1,1280]{2,1,0:T(1,128)}), f32[256,1,1280]{2,1,0:T(1,128)S(1)}, u32[]{:S(2)}, u32[]{:S(2)}) async-start(f32[256,1,1280]{2,1,0:T(1,128)} %bitcast.54), calls=%async_computation | async-start | bytes 2621440 | tf_op jit(solution)/shard_map/all_to_all | solution.py:331
  28.6 11.8 %collective-permute-start.1 = (f32[64,64]{0,1:T(8,128)S(1)}, f32[64,64]{0,1:T(8,128)S(1)}, u32[]{:S(2)}, u32[]{:S(2)}) collective-permute-start(f32[64,64]{0,1:T(8,128)S(1)} %constant_dynamic-slice_fusion), channel_id=1, source_target_pairs={{0,4},{4,0},{1,5},{5,1},{2,6},{6,2},{3,7},{7,3},{8,12},{12,8},{9,1... | collective-permute-start | bytes 49160 | tf_op jit(solution)/shard_map/ppermute | solution.py:44
  40.7 1.0 fusion.8
  42.6 2.6 %fusion.push_ref = f32[256,512]{1,0:T(8,128)S(1)} fusion(f32[2048]{0:T(1024)S(1)} %mul.78, s32[512]{0:T(512)S(1)} %fusion.25, s32[2048]{0:T(1024)S(1)} %copy-done.10, s32[2048]{0:T(1024)S(1)} %copy-done.11, s32[256]{0:T(256)S(1)} %compare_select_fusion), kind=kOutput, calls=%fused_computation | convolution fusion | flops 3223846912 | bytes 551936 | tf_op jit(solution)/shard_map/dot_general | solution.py:77
  45.2 1.0 fusion.12
  46.2 40.7 %collective-permute-done.1 = f32[64,64]{0,1:T(8,128)S(1)} collective-permute-done((f32[64,64]{0,1:T(8,128)S(1)}, f32[64,64]{0,1:T(8,128)S(1)}, u32[]{:S(2)}, u32[]{:S(2)}) %collective-permute-start.1) | collective-permute-done | bytes 16416 | tf_op jit(solution)/shard_map/ppermute | solution.py:44
  87.1 7.1 %collective-permute-start.2 = (f32[64,128]{0,1:T(8,128)S(1)}, f32[64,128]{0,1:T(8,128)S(1)}, u32[]{:S(2)}, u32[]{:S(2)}) collective-permute-start(f32[64,128]{0,1:T(8,128)S(1)} %get-tuple-element.23), channel_id=1, source_target_pairs={{0,8},{8,0},{1,9},{9,1},{2,10},{10,2},{3,11},{11,3},{4,12},{12,4},... | collective-permute-start | bytes 98312 | tf_op jit(solution)/shard_map/ppermute | solution.py:35
  95.2 3.1 %collective-permute-start.3 = (f32[2,64,128]{2,1,0:T(8,128)S(1)}, f32[2,64,128]{2,1,0:T(8,128)S(1)}, u32[]{:S(2)}, u32[]{:S(2)}) collective-permute-start(f32[2,64,128]{2,1,0:T(8,128)S(1)} %constant_dynamic-update-slice_fusion), channel_id=1, source_target_pairs={{0,16},{16,32},{32,48},{48,0},{1,17},{17,33},{33,49},{49,1},{2,18}... | collective-permute-start | bytes 196616 | tf_op jit(solution)/shard_map/ppermute | solution.py:35
  98.4 3.5 %collective-permute-start.4 = (f32[2,64,128]{2,1,0:T(8,128)S(1)}, f32[2,64,128]{2,1,0:T(8,128)S(1)}, u32[]{:S(2)}, u32[]{:S(2)}) collective-permute-start(f32[2,64,128]{2,1,0:T(8,128)S(1)} %constant_dynamic-update-slice_fusion), channel_id=1, source_target_pairs={{0,32},{16,48},{32,0},{48,16},{1,33},{17,49},{33,1},{49,17},{2,34}... | collective-permute-start | bytes 196616 | tf_op jit(solution)/shard_map/ppermute | solution.py:35
  101.9 1.9 collective-permute-start.5
  106.4 2.8 %collective-permute-start = (f32[2560,128]{1,0:T(8,128)S(1)}, f32[2560,128]{1,0:T(8,128)S(1)}, u32[]{:S(2)}, u32[]{:S(2)}) collective-permute-start(f32[2560,128]{1,0:T(8,128)S(1)} %bitcast.51), channel_id=1, source_target_pairs={{0,8},{8,0},{1,9},{9,1},{2,10},{10,2},{3,11},{11,3},{4,12},{12,4},... | collective-permute-start | bytes 3932168 | tf_op jit(solution)/shard_map/ppermute | solution.py:359
  109.9 1.9 collective-permute-start.6
  111.8 1.3 fusion.43.wz_ref
  113.2 5.3 %collective-permute-start.7 = (f32[4,2,64,128]{3,2,1,0:T(8,128)}, f32[4,2,64,128]{3,2,1,0:T(8,128)S(1)}, u32[]{:S(2)}, u32[]{:S(2)}) collective-permute-start(f32[4,2,64,128]{3,2,1,0:T(8,128)} %bitcast_dynamic-update-slice_fusion.4), channel_id=1, source_target_pairs={{0,2},{1,3},{2,0},{3,1},{4,6},{5,7},{6,4},{7,5},{8,10},{9,11},{10,... | collective-permute-start | bytes 786440 | tf_op jit(solution)/shard_map/ppermute | solution.py:35
  118.5 2.1 collective-permute-start.8
  120.7 1.0 bitcast_dynamic-update-slice_fusion.3
  121.7 1.0 bitcast_dynamic-update-slice_fusion.2
  122.7 4.2 %collective-permute-done.7 = f32[4,2,64,128]{3,2,1,0:T(8,128)S(1)} collective-permute-done((f32[4,2,64,128]{3,2,1,0:T(8,128)}, f32[4,2,64,128]{3,2,1,0:T(8,128)S(1)}, u32[]{:S(2)}, u32[]{:S(2)}) %collective-permute-start.7) | collective-permute-done | bytes 262176 | tf_op jit(solution)/shard_map/ppermute | solution.py:35
  127.0 3.0 %collective-permute-done.8 = f32[4,2,64,128]{3,2,1,0:T(8,128)S(1)} collective-permute-done((f32[4,2,64,128]{3,2,1,0:T(8,128)}, f32[4,2,64,128]{3,2,1,0:T(8,128)S(1)}, u32[]{:S(2)}, u32[]{:S(2)}) %collective-permute-start.8) | collective-permute-done | bytes 262176 | tf_op jit(solution)/shard_map/ppermute | solution.py:35
  130.2 2.8 %shard_map.111 = f32[2816,128]{1,0:T(8,128)S(1)} custom-call(f32[2560,128]{1,0:T(8,128)S(1)} %bitcast.52, f32[2560,128]{1,0:T(8,128)S(1)} %collective-permute-done.other_ref, f32[256,512]{1,0:T(8,128)S(1)} %fusion.push_ref, bf16[128,256]{1,0:T(8,128)(2,1)S(1)} %get-tuple-element.13.wz_high, bf16[128,256]{1,0:T(8,128)(2,1)S(1)} %get-tuple-element.14.wz_low, ...), custom_call_target="tpu_custom_call" | custom-call | flops 1509949440 | bytes 8388608 | tf_op jit(solution)/shard_map/pallas_call | solution.py:155
  133.0 1.1 copy-done.1
  134.2 16.2 %all-to-all-start.1 = ((f32[256,1,1408]{2,1,0:T(1,128)}), f32[256,1,1408]{2,1,0:T(1,128)S(1)}, u32[]{:S(2)}, u32[]{:S(2)}) async-start(f32[256,1,1408]{2,1,0:T(1,128)} %bitcast.50), calls=%async_computation.1 | async-start | bytes 2883584 | tf_op jit(solution)/shard_map/all_to_all | solution.py:331
  150.4 1.3 collective-permute-start.10
  151.7 4.0 %collective-permute-start.9 = (f32[4,256]{1,0:T(4,128)S(1)}, f32[4,256]{1,0:T(4,128)S(1)}, u32[]{:S(2)}, u32[]{:S(2)}) collective-permute-start(f32[4,256]{1,0:T(4,128)S(1)} %get-tuple-element.21), channel_id=1, source_target_pairs={{0,1},{1,2},{2,3},{3,4},{4,5},{5,6},{6,7},{8,9},{9,10},{10,11},{11... | collective-permute-start | bytes 12296 | tf_op jit(solution)/shard_map/ppermute | solution.py:325
  155.9 63.7 %all-to-all-done.1 = f32[256,1,1408]{2,1,0:T(1,128)S(1)} async-done(((f32[256,1,1408]{2,1,0:T(1,128)}), f32[256,1,1408]{2,1,0:T(1,128)S(1)}, u32[]{:S(2)}, u32[]{:S(2)}) %all-to-all-start.1) | async-done | bytes 1441824 | tf_op jit(solution)/shard_map/all_to_all | solution.py:331
  220.0 7.2 %collective-permute-start.11 = (f32[5,64,256]{2,1,0:T(8,128)S(1)}, f32[5,64,256]{2,1,0:T(8,128)S(1)}, u32[]{:S(2)}, u32[]{:S(2)}) collective-permute-start(f32[5,64,256]{2,1,0:T(8,128)S(1)} %get-tuple-element.19), channel_id=1, source_target_pairs={{0,8},{8,16},{16,24},{24,32},{32,40},{40,48},{48,56},{56,64},{64,7... | collective-permute-start | bytes 983048 | tf_op jit(solution)/shard_map/ppermute | solution.py:325
  227.2 1.9 collective-permute-start.12
  229.2 0.9 convert_bitcast_fusion.1.thick_ref
  230.1 1.3 shard_map.113.most_ref
  231.5 6.3 %collective-permute-done.12.above_ref = f32[5,64,256]{2,1,0:T(8,128)S(1)} collective-permute-done((f32[5,64,256]{2,1,0:T(8,128)S(1)}, f32[5,64,256]{2,1,0:T(8,128)S(1)}, u32[]{:S(2)}, u32[]{:S(2)}) %collective-permute-start.12) | collective-permute-done | bytes 327712 | tf_op jit(solution)/shard_map/ppermute | solution.py:326
  237.7 1.5 shard_map.114
  (64 shorter events, 6.3 us)
Async XLA Ops:
  0.0 45.2 %copy-start = (f32[256,256]{1,0:T(8,128)S(1)}, f32[256,256]{1,0:T(8,128)}, u32[]{:S(2)}) copy-start(f32[256,256]{1,0:T(8,128)} %param.21) | copy-start | bytes 786436
  5.3 23.2 %copy-start.5 = (f32[512,64]{0,1:T(8,128)S(1)}, f32[512,64]{0,1:T(8,128)}, u32[]{:S(2)}) copy-start(f32[512,64]{0,1:T(8,128)} %param.19) | copy-start | bytes 393220
  5.3 35.1 %copy-start.2 = (f32[256,256]{1,0:T(8,128)S(1)}, f32[256,256]{1,0:T(8,128)}, u32[]{:S(2)}) copy-start(f32[256,256]{1,0:T(8,128)} %inv_ref.1) | copy-start | bytes 786436
  5.3 35.3 %copy-start.9 = (s32[2048]{0:T(1024)S(1)}, s32[2048]{0:T(1024)}, u32[]{:S(2)}) copy-start(s32[2048]{0:T(1024)} %param.17) | copy-start | bytes 24580
  5.3 36.4 %copy-start.6 = (f32[2048]{0:T(1024)S(1)}, f32[2048]{0:T(1024)}, u32[]{:S(2)}) copy-start(f32[2048]{0:T(1024)} %param.18) | copy-start | bytes 24580
  5.4 37.2 %copy-start.10 = (s32[2048]{0:T(1024)S(1)}, s32[2048]{0:T(1024)}, u32[]{:S(2)}) copy-start(s32[2048]{0:T(1024)} %param.15) | copy-start | bytes 24580
  5.4 37.2 %copy-start.11 = (s32[2048]{0:T(1024)S(1)}, s32[2048]{0:T(1024)}, u32[]{:S(2)}) copy-start(s32[2048]{0:T(1024)} %param.16) | copy-start | bytes 24580
  5.4 101.1 %all-to-all-start = ((f32[256,1,1280]{2,1,0:T(1,128)}), f32[256,1,1280]{2,1,0:T(1,128)S(1)}, u32[]{:S(2)}, u32[]{:S(2)}) async-start(f32[256,1,1280]{2,1,0:T(1,128)} %bitcast.54), calls=%async_computation | async-start | bytes 2621440 | tf_op jit(solution)/shard_map/all_to_all | solution.py:331
  28.6 58.3 %collective-permute-start.1 = (f32[64,64]{0,1:T(8,128)S(1)}, f32[64,64]{0,1:T(8,128)S(1)}, u32[]{:S(2)}, u32[]{:S(2)}) collective-permute-start(f32[64,64]{0,1:T(8,128)S(1)} %constant_dynamic-slice_fusion), channel_id=1, source_target_pairs={{0,4},{4,0},{1,5},{5,1},{2,6},{6,2},{3,7},{7,3},{8,12},{12,8},{9,1... | collective-permute-start | bytes 49160 | tf_op jit(solution)/shard_map/ppermute | solution.py:44
  41.8 0.5 copy-start.7
  41.8 0.6 copy-start.8
  87.1 8.0 %collective-permute-start.2 = (f32[64,128]{0,1:T(8,128)S(1)}, f32[64,128]{0,1:T(8,128)S(1)}, u32[]{:S(2)}, u32[]{:S(2)}) collective-permute-start(f32[64,128]{0,1:T(8,128)S(1)} %get-tuple-element.23), channel_id=1, source_target_pairs={{0,8},{8,0},{1,9},{9,1},{2,10},{10,2},{3,11},{11,3},{4,12},{12,4},... | collective-permute-start | bytes 98312 | tf_op jit(solution)/shard_map/ppermute | solution.py:35
  95.2 10.0 %collective-permute-start.3 = (f32[2,64,128]{2,1,0:T(8,128)S(1)}, f32[2,64,128]{2,1,0:T(8,128)S(1)}, u32[]{:S(2)}, u32[]{:S(2)}) collective-permute-start(f32[2,64,128]{2,1,0:T(8,128)S(1)} %constant_dynamic-update-slice_fusion), channel_id=1, source_target_pairs={{0,16},{16,32},{32,48},{48,0},{1,17},{17,33},{33,49},{49,1},{2,18}... | collective-permute-start | bytes 196616 | tf_op jit(solution)/shard_map/ppermute | solution.py:35
  98.4 7.4 %collective-permute-start.4 = (f32[2,64,128]{2,1,0:T(8,128)S(1)}, f32[2,64,128]{2,1,0:T(8,128)S(1)}, u32[]{:S(2)}, u32[]{:S(2)}) collective-permute-start(f32[2,64,128]{2,1,0:T(8,128)S(1)} %constant_dynamic-update-slice_fusion), channel_id=1, source_target_pairs={{0,32},{16,48},{32,0},{48,16},{1,33},{17,49},{33,1},{49,17},{2,34}... | collective-permute-start | bytes 196616 | tf_op jit(solution)/shard_map/ppermute | solution.py:35
  101.9 7.3 %collective-permute-start.5 = (f32[2,64,128]{2,1,0:T(8,128)S(1)}, f32[2,64,128]{2,1,0:T(8,128)S(1)}, u32[]{:S(2)}, u32[]{:S(2)}) collective-permute-start(f32[2,64,128]{2,1,0:T(8,128)S(1)} %constant_dynamic-update-slice_fusion), channel_id=1, source_target_pairs={{0,48},{16,0},{32,16},{48,32},{1,49},{17,1},{33,17},{49,33},{2,50}... | collective-permute-start | bytes 196616 | tf_op jit(solution)/shard_map/ppermute | solution.py:35
  106.4 23.7 %collective-permute-start = (f32[2560,128]{1,0:T(8,128)S(1)}, f32[2560,128]{1,0:T(8,128)S(1)}, u32[]{:S(2)}, u32[]{:S(2)}) collective-permute-start(f32[2560,128]{1,0:T(8,128)S(1)} %bitcast.51), channel_id=1, source_target_pairs={{0,8},{8,0},{1,9},{9,1},{2,10},{10,2},{3,11},{11,3},{4,12},{12,4},... | collective-permute-start | bytes 3932168 | tf_op jit(solution)/shard_map/ppermute | solution.py:359
  109.9 11.8 %collective-permute-start.6 = (f32[4,2,64,128]{3,2,1,0:T(8,128)}, f32[4,2,64,128]{3,2,1,0:T(8,128)}, u32[]{:S(2)}, u32[]{:S(2)}) collective-permute-start(f32[4,2,64,128]{3,2,1,0:T(8,128)} %bitcast_dynamic-update-slice_fusion.4), channel_id=1, source_target_pairs={{0,1},{1,2},{2,3},{3,0},{4,5},{5,6},{6,7},{7,4},{8,9},{9,10},{10,1... | collective-permute-start | bytes 786440 | tf_op jit(solution)/shard_map/ppermute | solution.py:35
  113.2 13.8 %collective-permute-start.7 = (f32[4,2,64,128]{3,2,1,0:T(8,128)}, f32[4,2,64,128]{3,2,1,0:T(8,128)S(1)}, u32[]{:S(2)}, u32[]{:S(2)}) collective-permute-start(f32[4,2,64,128]{3,2,1,0:T(8,128)} %bitcast_dynamic-update-slice_fusion.4), channel_id=1, source_target_pairs={{0,2},{1,3},{2,0},{3,1},{4,6},{5,7},{6,4},{7,5},{8,10},{9,11},{10,... | collective-permute-start | bytes 786440 | tf_op jit(solution)/shard_map/ppermute | solution.py:35
  118.5 11.5 %collective-permute-start.8 = (f32[4,2,64,128]{3,2,1,0:T(8,128)}, f32[4,2,64,128]{3,2,1,0:T(8,128)S(1)}, u32[]{:S(2)}, u32[]{:S(2)}) collective-permute-start(f32[4,2,64,128]{3,2,1,0:T(8,128)} %bitcast_dynamic-update-slice_fusion.4), channel_id=1, source_target_pairs={{0,3},{1,0},{2,1},{3,2},{4,7},{5,4},{6,5},{7,6},{8,11},{9,8},{10,9... | collective-permute-start | bytes 786440 | tf_op jit(solution)/shard_map/ppermute | solution.py:35
  133.0 1.1 copy-start.1
  134.1 16.2 %copy-start.4 = (s32[64,4,256]{2,1,0:T(4,128)S(1)}, s32[64,4,256]{2,1,0:T(4,128)}, u32[]{:S(2)}) copy-start(s32[64,4,256]{2,1,0:T(4,128)} %param.14) | copy-start | bytes 786436
  134.1 21.6 %copy-start.3 = (bf16[3,64,4,256]{3,2,1,0:T(4,128)(2,1)S(1)}, bf16[3,64,4,256]{3,2,1,0:T(4,128)(2,1)}, u32[]{:S(2)}) copy-start(bf16[3,64,4,256]{3,2,1,0:T(4,128)(2,1)} %param.12) | copy-start | bytes 1179652
  134.2 85.5 %all-to-all-start.1 = ((f32[256,1,1408]{2,1,0:T(1,128)}), f32[256,1,1408]{2,1,0:T(1,128)S(1)}, u32[]{:S(2)}, u32[]{:S(2)}) async-start(f32[256,1,1408]{2,1,0:T(1,128)} %bitcast.50), calls=%async_computation.1 | async-start | bytes 2883584 | tf_op jit(solution)/shard_map/all_to_all | solution.py:331
  150.4 79.7 %collective-permute-start.10 = (f32[4,256]{1,0:T(4,128)S(1)}, f32[4,256]{1,0:T(4,128)S(1)}, u32[]{:S(2)}, u32[]{:S(2)}) collective-permute-start(f32[4,256]{1,0:T(4,128)S(1)} %get-tuple-element.22), channel_id=1, source_target_pairs={{1,0},{2,1},{3,2},{4,3},{5,4},{6,5},{7,6},{9,8},{10,9},{11,10},{12... | collective-permute-start | bytes 12296 | tf_op jit(solution)/shard_map/ppermute | solution.py:326
  151.7 78.4 %collective-permute-start.9 = (f32[4,256]{1,0:T(4,128)S(1)}, f32[4,256]{1,0:T(4,128)S(1)}, u32[]{:S(2)}, u32[]{:S(2)}) collective-permute-start(f32[4,256]{1,0:T(4,128)S(1)} %get-tuple-element.21), channel_id=1, source_target_pairs={{0,1},{1,2},{2,3},{3,4},{4,5},{5,6},{6,7},{8,9},{9,10},{10,11},{11... | collective-permute-start | bytes 12296 | tf_op jit(solution)/shard_map/ppermute | solution.py:325
  220.0 11.4 %collective-permute-start.11 = (f32[5,64,256]{2,1,0:T(8,128)S(1)}, f32[5,64,256]{2,1,0:T(8,128)S(1)}, u32[]{:S(2)}, u32[]{:S(2)}) collective-permute-start(f32[5,64,256]{2,1,0:T(8,128)S(1)} %get-tuple-element.19), channel_id=1, source_target_pairs={{0,8},{8,16},{16,24},{24,32},{32,40},{40,48},{48,56},{56,64},{64,7... | collective-permute-start | bytes 983048 | tf_op jit(solution)/shard_map/ppermute | solution.py:325
  227.2 10.5 %collective-permute-start.12 = (f32[5,64,256]{2,1,0:T(8,128)S(1)}, f32[5,64,256]{2,1,0:T(8,128)S(1)}, u32[]{:S(2)}, u32[]{:S(2)}) collective-permute-start(f32[5,64,256]{2,1,0:T(8,128)S(1)} %get-tuple-element.20), channel_id=1, source_target_pairs={{8,0},{16,8},{24,16},{32,24},{40,32},{48,40},{56,48},{64,56},{72,6... | collective-permute-start | bytes 983048 | tf_op jit(solution)/shard_map/ppermute | solution.py:326

commit v3 on v2

--- a/solution.py
+++ b/solution.py
@@ -47,9 +47,9 @@
 
 
 def whole_inv_x(pair):
-    for axis in ("co", "xx", "yy"):
+    for axis in ("xx", "yy", "co"):
         pair = gather_ring(pair, axis)
-    return pair.reshape(pair.shape[0], -1, pair.shape[-1])
+    return pair.reshape(*pair.shape[:2], -1, pair.shape[-1])
 
 
 def z_of(k, which, half, z_rows):
@@ -165,23 +165,20 @@
     )(own, other, push, *weights)
 
 
-def y_kernel(fields, cells_ref, inv_ref, out_ref, high_ref, low_ref):
-    c = pl.program_id(0)
-
-    @pl.when(c == 0)
-    def _():
-        high_ref[...], low_ref[...] = parts(inv_ref[...].T)
-
+def y_kernel(fields, cells_ref, inv_ref, out_ref):
+    inv = parts(inv_ref[...].T)
+    rows = 2 * fields
     contract = (((1,), (1,)), ((), ()))
     dot = lambda a, b: lax.dot_general(a, b, contract, preferred_element_type=jnp.float32)
-    for pair in range(2):
-        both = []
-        for z in (2 * pair, 2 * pair + 1):
-            tiles = [cells_ref[pl.ds(4 * tile + z, 64, stride=8), :] for tile in range(2)]
-            both.append(jnp.concatenate(tiles, axis=1))
-        high, low = parts(jnp.concatenate(both, axis=0))
-        done = dot(high_ref[...], high) + (dot(high_ref[...], low) + dot(low_ref[...], high))
-        out_ref[pl.ds(2 * c + pair, 256, stride=2 * fields), :] = done
+    for c in range(fields):
+        for pair in range(2):
+            both = []
+            for z in (2 * pair, 2 * pair + 1):
+                tiles = [cells_ref[pl.ds(c * 512 + 4 * tile + z, 64, stride=8), :] for tile in range(2)]
+                both.append(jnp.concatenate(tiles, axis=1))
+            high, low = parts(jnp.concatenate(both, axis=0))
+            done = dot(inv[0], high) + (dot(inv[0], low) + dot(inv[1], high))
+            out_ref[pl.ds(2 * c + pair, 256, stride=rows), :] = done
 
 
 def y_solved(cells, inv_y):
@@ -189,15 +186,10 @@
     tiles = cells.reshape(fields, x_rows, z_rows, y_cells // 128, 128).transpose(0, 1, 3, 2, 4).reshape(-1, 128)
     return pl.pallas_call(
         functools.partial(y_kernel, fields),
-        grid=(fields,),
         out_shape=jax.ShapeDtypeStruct(tiles.shape, jnp.float32),
-        in_specs=[
-            pl.BlockSpec((tiles.shape[0] // fields, 128), lambda c: (c, 0)),
-            pl.BlockSpec(inv_y.shape, lambda c: (0, 0)),
-        ],
-        out_specs=pl.BlockSpec(tiles.shape, lambda c: (0, 0)),
-        scratch_shapes=[pltpu.VMEM(inv_y.shape, jnp.bfloat16)] * 2,
-        compiler_params=pltpu.CompilerParams(vmem_limit_bytes=61000 * 1024),
+        in_specs=[vmem] * 2,
+        out_specs=vmem,
+        compiler_params=params,
         cost_estimate=pl.CostEstimate(flops=6 * tiles.size * y_cells, bytes_accessed=3 * 2**20, transcendentals=0),
     )(tiles, inv_y)
 
@@ -207,14 +199,14 @@
     for yy in range(4):
         for zh in range(2):
             j = zh * 4 + yy
-            rows = jnp.concatenate([ix_ref[q, pl.ds(64 * j, 64), :] for q in range(4)], axis=1)
+            rows = jnp.concatenate([ix_ref[j % 2, q, pl.ds(64 * (j // 2), 64), :] for q in range(4)], axis=1)
             at = pl.ds(64 * (2 * yy + zh), 64)
             ix_high[at, :], ix_low[at, :] = parts(rows)
 
 
 def prepared(wz, ix):
     half = lambda shape: jax.ShapeDtypeStruct(shape, jnp.bfloat16)
-    count = ix.shape[1]
+    count = ix.shape[0] * ix.shape[2]
     return pl.pallas_call(
         weights_kernel,
         out_shape=(half(wz.shape), half(wz.shape), half((count, count)), half((count, count))),

time: 240 us -> 239 us (level)
  local copies, waits for them, and re-layouts: 7.49 us -> 11.2 us
  Pallas kernels: 11.5 us -> 8.46 us
    ppermute x1, starting transfers between devices: 2.82 us -> 9.74 us  [body(): other = lax.ppermute(got, 'co', swap)]
    ppermute x7, waiting for transfers between devices: 8.1 us -> 2.26 us  [gather_ring(): lax.ppermute(block, axis, [(i, (i + hop) % count) for i in range(count)])]
    ppermute x7, starting transfers between devices: 25.1 us -> 21 us  [gather_ring(): lax.ppermute(block, axis, [(i, (i + hop) % count) for i in range(count)])]
    pallas_call x1, Pallas kernels: 5.33 us -> 2.3 us  [y_solved(): pl.pallas_call(functools.partial(y_kernel, fields), out_shape=jax.ShapeDt...]
    ppermute x1, waiting for transfers between devices: 40.7 us -> 43.8 us  [inv_x_pair(): theirs = lax.ppermute(mine, 'zh', swap)]
  transfers between devices with their start and end apart: 15 -> 15, of which waited for: 6 -> 6; matrix products, arithmetic and copies ran while one was open for 5% -> 6% of each run, Pallas kernels for 1% -> 1%
where the time goes in v3:
time: 239 us
  waiting for transfers between devices  117 us (49%)
  starting transfers between devices  94.9 us (40%)
  local copies, waits for them, and re-layouts  11.2 us (5%)
  Pallas kernels  8.46 us (4%)
  matrix products  5.03 us (2%)
    all_to_all x2, waiting for transfers between devices, transposed(): return lax.all_to_all(sent, chips, split_axis=0, concat_axis=0, tiled=True)  63.7 us
    ppermute x1, waiting for transfers between devices, inv_x_pair(): theirs = lax.ppermute(mine, 'zh', swap)  43.8 us
    all_to_all x2, starting transfers between devices, transposed(): return lax.all_to_all(sent, chips, split_axis=0, concat_axis=0, tiled=True)  38.2 us
    ppermute x7, starting transfers between devices, gather_ring(): lax.ppermute(block, axis, [(i, (i + hop) % count) for i in range(count)])  21 us
    ppermute x1, starting transfers between devices, inv_x_pair(): theirs = lax.ppermute(mine, 'zh', swap)  11.8 us
    ppermute x2, starting transfers between devices, before_and_after(): before = lax.ppermute(tail, axes, [(i, i + 1) for i in range(count - 1)])  10.9 us
    ppermute x1, starting transfers between devices, body(): other = lax.ppermute(got, 'co', swap)  9.74 us
    ppermute x2, waiting for transfers between devices, before_and_after(): after = lax.ppermute(head, axes, [(i + 1, i) for i in range(count - 1)])  6.51 us
  transfers between devices with their start and end apart: 15, of which 6 were waited for; matrix products, arithmetic and copies ran while one was open for 6% of the time, Pallas kernels for 1%

profile of v3, /device:TPU:7, one launch (start us, length us, event | category | flops | bytes accessed | tf_op | source)
XLA Modules:
  0.0 238.7 jit_solution(5160660623122513521)
XLA Ops:
  0.0 1.4 copy-done.2
  1.4 0.9 copy-done.3
  2.3 2.3 shard_map.109
  4.6 23.1 %all-to-all-start = ((f32[256,1,1280]{2,1,0:T(1,128)}), f32[256,1,1280]{2,1,0:T(1,128)S(1)}, u32[]{:S(2)}, u32[]{:S(2)}) async-start(f32[256,1,1280]{2,1,0:T(1,128)} %bitcast.3), calls=%async_computation | async-start | bytes 2621440 | tf_op jit(solution)/shard_map/all_to_all | solution.py:323
  27.9 11.8 %collective-permute-start.1 = (f32[64,64]{0,1:T(8,128)S(1)}, f32[64,64]{0,1:T(8,128)S(1)}, u32[]{:S(2)}, u32[]{:S(2)}) collective-permute-start(f32[64,64]{0,1:T(8,128)S(1)} %constant_dynamic-slice_fusion), channel_id=1, source_target_pairs={{0,4},{4,0},{1,5},{5,1},{2,6},{6,2},{3,7},{7,3},{8,12},{12,8},{9,1... | collective-permute-start | bytes 49160 | tf_op jit(solution)/shard_map/ppermute | solution.py:44
  39.9 1.0 fusion.8
  42.4 43.8 %collective-permute-done.1 = f32[64,64]{0,1:T(8,128)S(1)} collective-permute-done((f32[64,64]{0,1:T(8,128)S(1)}, f32[64,64]{0,1:T(8,128)S(1)}, u32[]{:S(2)}, u32[]{:S(2)}) %collective-permute-start.1) | collective-permute-done | bytes 16416 | tf_op jit(solution)/shard_map/ppermute | solution.py:44
  86.3 4.8 %collective-permute-start.2 = (f32[64,128]{0,1:T(8,128)S(1)}, f32[64,128]{0,1:T(8,128)S(1)}, u32[]{:S(2)}, u32[]{:S(2)}) collective-permute-start(f32[64,128]{0,1:T(8,128)S(1)} %get-tuple-element.23), channel_id=1, source_target_pairs={{0,16},{16,32},{32,48},{48,0},{1,17},{17,33},{33,49},{49,1},{2,18}... | collective-permute-start | bytes 98312 | tf_op jit(solution)/shard_map/ppermute | solution.py:35
  91.1 1.9 collective-permute-start.3
  93.0 2.5 %collective-permute-start.4 = (f32[64,128]{0,1:T(8,128)S(1)}, f32[64,128]{0,1:T(8,128)S(1)}, u32[]{:S(2)}, u32[]{:S(2)}) collective-permute-start(f32[64,128]{0,1:T(8,128)S(1)} %get-tuple-element.23), channel_id=1, source_target_pairs={{0,48},{16,0},{32,16},{48,32},{1,49},{17,1},{33,17},{49,33},{2,50}... | collective-permute-start | bytes 98312 | tf_op jit(solution)/shard_map/ppermute | solution.py:35
  97.6 1.6 collective-permute-done.4
  101.1 1.9 collective-permute-start.5
  103.0 4.5 %collective-permute-start.6 = (f32[4,64,128]{2,1,0:T(8,128)}, f32[4,64,128]{2,1,0:T(8,128)}, u32[]{:S(2)}, u32[]{:S(2)}) collective-permute-start(f32[4,64,128]{2,1,0:T(8,128)} %constant_dynamic-update-slice_fusion), channel_id=1, source_target_pairs={{0,2},{1,3},{2,0},{3,1},{4,6},{5,7},{6,4},{7,5},{8,10},{9,11},{10,... | collective-permute-start | bytes 393224 | tf_op jit(solution)/shard_map/ppermute | solution.py:35
  107.6 2.0 collective-permute-start.7
  109.6 0.9 bitcast_dynamic-update-slice_fusion.5
  110.6 9.7 %collective-permute-start = (f32[2560,128]{1,0:T(8,128)S(1)}, f32[2560,128]{1,0:T(8,128)S(1)}, u32[]{:S(2)}, u32[]{:S(2)}) collective-permute-start(f32[2560,128]{1,0:T(8,128)S(1)} %bitcast.49), channel_id=1, source_target_pairs={{0,8},{8,0},{1,9},{9,1},{2,10},{10,2},{3,11},{11,3},{4,12},{12,4},... | collective-permute-start | bytes 3932168 | tf_op jit(solution)/shard_map/ppermute | solution.py:351
  120.3 0.9 bitcast_dynamic-update-slice_fusion.3
  121.3 0.9 bitcast_dynamic-update-slice_fusion.2
  122.2 3.5 %collective-permute-start.8 = (f32[4,4,64,128]{3,2,1,0:T(8,128)S(1)}, f32[4,4,64,128]{3,2,1,0:T(8,128)}, u32[]{:S(2)}, u32[]{:S(2)}) collective-permute-start(f32[4,4,64,128]{3,2,1,0:T(8,128)S(1)} %bitcast_dynamic-update-slice_fusion.2), channel_id=1, source_target_pairs={{0,8},{8,0},{1,9},{9,1},{2,10},{10,2},{3,11},{11,3},{4,12},{12,4},... | collective-permute-start | bytes 1572872 | tf_op jit(solution)/shard_map/ppermute | solution.py:35
  126.2 3.4 %fusion.push_ref = f32[256,512]{1,0:T(8,128)S(1)} fusion(f32[2048]{0:T(1024)S(1)} %mul.78, s32[512]{0:T(512)} %fusion.25, s32[2048]{0:T(1024)} %param.15, s32[2048]{0:T(1024)} %param.16, s32[256]{0:T(256)} %compare_select_fusion), kind=kOutput, calls=%fused_computation | convolution fusion | flops 3223846912 | bytes 551936 | tf_op jit(solution)/shard_map/dot_general | solution.py:77
  129.8 1.1 bitcast_dynamic-update-slice_fusion
  131.0 2.8 %shard_map.111 = f32[2816,128]{1,0:T(8,128)S(1)} custom-call(f32[2560,128]{1,0:T(8,128)S(1)} %bitcast.50, f32[2560,128]{1,0:T(8,128)S(1)} %collective-permute-done.other_ref, f32[256,512]{1,0:T(8,128)S(1)} %fusion.push_ref, bf16[128,256]{1,0:T(8,128)(2,1)S(1)} %get-tuple-element.13.wz_high, bf16[128,256]{1,0:T(8,128)(2,1)S(1)} %get-tuple-element.14.wz_low, ...), custom_call_target="tpu_custom_call" | custom-call | flops 1509949440 | bytes 8388608 | tf_op jit(solution)/shard_map/pallas_call | solution.py:155
  133.9 1.1 copy-done.1
  135.0 15.1 %all-to-all-start.1 = ((f32[256,1,1408]{2,1,0:T(1,128)}), f32[256,1,1408]{2,1,0:T(1,128)S(1)}, u32[]{:S(2)}, u32[]{:S(2)}) async-start(f32[256,1,1408]{2,1,0:T(1,128)} %bitcast.48), calls=%async_computation.1 | async-start | bytes 2883584 | tf_op jit(solution)/shard_map/all_to_all | solution.py:323
  150.2 1.3 collective-permute-start.10
  151.5 4.0 %collective-permute-start.9 = (f32[4,256]{1,0:T(4,128)S(1)}, f32[4,256]{1,0:T(4,128)S(1)}, u32[]{:S(2)}, u32[]{:S(2)}) collective-permute-start(f32[4,256]{1,0:T(4,128)S(1)} %get-tuple-element.21), channel_id=1, source_target_pairs={{0,1},{1,2},{2,3},{3,4},{4,5},{5,6},{6,7},{8,9},{9,10},{10,11},{11... | collective-permute-start | bytes 12296 | tf_op jit(solution)/shard_map/ppermute | solution.py:317
  155.7 63.7 %all-to-all-done.1 = f32[256,1,1408]{2,1,0:T(1,128)S(1)} async-done(((f32[256,1,1408]{2,1,0:T(1,128)}), f32[256,1,1408]{2,1,0:T(1,128)S(1)}, u32[]{:S(2)}, u32[]{:S(2)}) %all-to-all-start.1) | async-done | bytes 1441824 | tf_op jit(solution)/shard_map/all_to_all | solution.py:323
  219.8 6.9 %collective-permute-start.11 = (f32[5,64,256]{2,1,0:T(8,128)S(1)}, f32[5,64,256]{2,1,0:T(8,128)S(1)}, u32[]{:S(2)}, u32[]{:S(2)}) collective-permute-start(f32[5,64,256]{2,1,0:T(8,128)S(1)} %get-tuple-element.19), channel_id=1, source_target_pairs={{0,8},{8,16},{16,24},{24,32},{32,40},{40,48},{48,56},{56,64},{64,7... | collective-permute-start | bytes 983048 | tf_op jit(solution)/shard_map/ppermute | solution.py:317
  226.7 1.9 collective-permute-start.12
  228.7 1.3 shard_map.113.most_ref
  230.7 6.5 %collective-permute-done.12.above_ref = f32[5,64,256]{2,1,0:T(8,128)S(1)} collective-permute-done((f32[5,64,256]{2,1,0:T(8,128)S(1)}, f32[5,64,256]{2,1,0:T(8,128)S(1)}, u32[]{:S(2)}, u32[]{:S(2)}) %collective-permute-start.12) | collective-permute-done | bytes 327712 | tf_op jit(solution)/shard_map/ppermute | solution.py:318
  237.2 1.5 shard_map.114
  (64 shorter events, 8.1 us)
Async XLA Ops:
  0.0 41.2 %copy-start = (f32[256,256]{1,0:T(8,128)S(1)}, f32[256,256]{1,0:T(8,128)}, u32[]{:S(2)}) copy-start(f32[256,256]{1,0:T(8,128)} %param.21) | copy-start | bytes 786436
  0.0 1.4 copy-start.2
  1.4 0.9 copy-start.3
  4.6 23.1 %copy-start.8 = (f32[512,64]{0,1:T(8,128)S(1)}, f32[512,64]{0,1:T(8,128)}, u32[]{:S(2)}) copy-start(f32[512,64]{0,1:T(8,128)} %param.19) | copy-start | bytes 393220
  4.6 35.1 %copy-start.4 = (f32[256,256]{1,0:T(8,128)S(1)}, f32[256,256]{1,0:T(8,128)}, u32[]{:S(2)}) copy-start(f32[256,256]{1,0:T(8,128)} %inv_ref.1) | copy-start | bytes 786436
  4.6 35.3 %copy-start.10 = (s32[2048]{0:T(1024)S(1)}, s32[2048]{0:T(1024)}, u32[]{:S(2)}) copy-start(s32[2048]{0:T(1024)} %param.17) | copy-start | bytes 24580
  4.6 105.9 %all-to-all-start = ((f32[256,1,1280]{2,1,0:T(1,128)}), f32[256,1,1280]{2,1,0:T(1,128)S(1)}, u32[]{:S(2)}, u32[]{:S(2)}) async-start(f32[256,1,1280]{2,1,0:T(1,128)} %bitcast.3), calls=%async_computation | async-start | bytes 2621440 | tf_op jit(solution)/shard_map/all_to_all | solution.py:323
  27.9 58.3 %collective-permute-start.1 = (f32[64,64]{0,1:T(8,128)S(1)}, f32[64,64]{0,1:T(8,128)S(1)}, u32[]{:S(2)}, u32[]{:S(2)}) collective-permute-start(f32[64,64]{0,1:T(8,128)S(1)} %constant_dynamic-slice_fusion), channel_id=1, source_target_pairs={{0,4},{4,0},{1,5},{5,1},{2,6},{6,2},{3,7},{7,3},{8,12},{12,8},{9,1... | collective-permute-start | bytes 49160 | tf_op jit(solution)/shard_map/ppermute | solution.py:44
  42.4 83.8 %copy-start.9 = (f32[2048]{0:T(1024)S(1)}, f32[2048]{0:T(1024)}, u32[]{:S(2)}) copy-start(f32[2048]{0:T(1024)} %param.18) | copy-start | bytes 24580
  86.3 10.6 %collective-permute-start.2 = (f32[64,128]{0,1:T(8,128)S(1)}, f32[64,128]{0,1:T(8,128)S(1)}, u32[]{:S(2)}, u32[]{:S(2)}) collective-permute-start(f32[64,128]{0,1:T(8,128)S(1)} %get-tuple-element.23), channel_id=1, source_target_pairs={{0,16},{16,32},{32,48},{48,0},{1,17},{17,33},{33,49},{49,1},{2,18}... | collective-permute-start | bytes 98312 | tf_op jit(solution)/shard_map/ppermute | solution.py:35
  91.1 6.5 %collective-permute-start.3 = (f32[64,128]{0,1:T(8,128)S(1)}, f32[64,128]{0,1:T(8,128)S(1)}, u32[]{:S(2)}, u32[]{:S(2)}) collective-permute-start(f32[64,128]{0,1:T(8,128)S(1)} %get-tuple-element.23), channel_id=1, source_target_pairs={{0,32},{16,48},{32,0},{48,16},{1,33},{17,49},{33,1},{49,17},{2,34}... | collective-permute-start | bytes 98312 | tf_op jit(solution)/shard_map/ppermute | solution.py:35
  93.0 6.2 %collective-permute-start.4 = (f32[64,128]{0,1:T(8,128)S(1)}, f32[64,128]{0,1:T(8,128)S(1)}, u32[]{:S(2)}, u32[]{:S(2)}) collective-permute-start(f32[64,128]{0,1:T(8,128)S(1)} %get-tuple-element.23), channel_id=1, source_target_pairs={{0,48},{16,0},{32,16},{48,32},{1,49},{17,1},{33,17},{49,33},{2,50}... | collective-permute-start | bytes 98312 | tf_op jit(solution)/shard_map/ppermute | solution.py:35
  101.1 9.4 %collective-permute-start.5 = (f32[4,64,128]{2,1,0:T(8,128)}, f32[4,64,128]{2,1,0:T(8,128)S(1)}, u32[]{:S(2)}, u32[]{:S(2)}) collective-permute-start(f32[4,64,128]{2,1,0:T(8,128)} %constant_dynamic-update-slice_fusion), channel_id=1, source_target_pairs={{0,1},{1,2},{2,3},{3,0},{4,5},{5,6},{6,7},{7,4},{8,9},{9,10},{10,1... | collective-permute-start | bytes 393224 | tf_op jit(solution)/shard_map/ppermute | solution.py:35
  103.0 17.3 %collective-permute-start.6 = (f32[4,64,128]{2,1,0:T(8,128)}, f32[4,64,128]{2,1,0:T(8,128)}, u32[]{:S(2)}, u32[]{:S(2)}) collective-permute-start(f32[4,64,128]{2,1,0:T(8,128)} %constant_dynamic-update-slice_fusion), channel_id=1, source_target_pairs={{0,2},{1,3},{2,0},{3,1},{4,6},{5,7},{6,4},{7,5},{8,10},{9,11},{10,... | collective-permute-start | bytes 393224 | tf_op jit(solution)/shard_map/ppermute | solution.py:35
  107.6 13.7 %collective-permute-start.7 = (f32[4,64,128]{2,1,0:T(8,128)}, f32[4,64,128]{2,1,0:T(8,128)}, u32[]{:S(2)}, u32[]{:S(2)}) collective-permute-start(f32[4,64,128]{2,1,0:T(8,128)} %constant_dynamic-update-slice_fusion), channel_id=1, source_target_pairs={{0,3},{1,0},{2,1},{3,2},{4,7},{5,4},{6,5},{7,6},{8,11},{9,8},{10,9... | collective-permute-start | bytes 393224 | tf_op jit(solution)/shard_map/ppermute | solution.py:35
  110.6 20.5 %collective-permute-start = (f32[2560,128]{1,0:T(8,128)S(1)}, f32[2560,128]{1,0:T(8,128)S(1)}, u32[]{:S(2)}, u32[]{:S(2)}) collective-permute-start(f32[2560,128]{1,0:T(8,128)S(1)} %bitcast.49), channel_id=1, source_target_pairs={{0,8},{8,0},{1,9},{9,1},{2,10},{10,2},{3,11},{11,3},{4,12},{12,4},... | collective-permute-start | bytes 3932168 | tf_op jit(solution)/shard_map/ppermute | solution.py:351
  122.2 7.6 %collective-permute-start.8 = (f32[4,4,64,128]{3,2,1,0:T(8,128)S(1)}, f32[4,4,64,128]{3,2,1,0:T(8,128)}, u32[]{:S(2)}, u32[]{:S(2)}) collective-permute-start(f32[4,4,64,128]{3,2,1,0:T(8,128)S(1)} %bitcast_dynamic-update-slice_fusion.2), channel_id=1, source_target_pairs={{0,8},{8,0},{1,9},{9,1},{2,10},{10,2},{3,11},{11,3},{4,12},{12,4},... | collective-permute-start | bytes 1572872 | tf_op jit(solution)/shard_map/ppermute | solution.py:35
  133.9 1.1 copy-start.1
  135.0 15.1 %copy-start.6 = (s32[64,4,256]{2,1,0:T(4,128)S(1)}, s32[64,4,256]{2,1,0:T(4,128)}, u32[]{:S(2)}) copy-start(s32[64,4,256]{2,1,0:T(4,128)} %param.14) | copy-start | bytes 786436
  135.0 20.5 %copy-start.5 = (bf16[3,64,4,256]{3,2,1,0:T(4,128)(2,1)S(1)}, bf16[3,64,4,256]{3,2,1,0:T(4,128)(2,1)}, u32[]{:S(2)}) copy-start(bf16[3,64,4,256]{3,2,1,0:T(4,128)(2,1)} %param.12) | copy-start | bytes 1179652
  135.0 84.4 %all-to-all-start.1 = ((f32[256,1,1408]{2,1,0:T(1,128)}), f32[256,1,1408]{2,1,0:T(1,128)S(1)}, u32[]{:S(2)}, u32[]{:S(2)}) async-start(f32[256,1,1408]{2,1,0:T(1,128)} %bitcast.48), calls=%async_computation.1 | async-start | bytes 2883584 | tf_op jit(solution)/shard_map/all_to_all | solution.py:323
  150.2 78.5 %collective-permute-start.10 = (f32[4,256]{1,0:T(4,128)S(1)}, f32[4,256]{1,0:T(4,128)S(1)}, u32[]{:S(2)}, u32[]{:S(2)}) collective-permute-start(f32[4,256]{1,0:T(4,128)S(1)} %get-tuple-element.22), channel_id=1, source_target_pairs={{1,0},{2,1},{3,2},{4,3},{5,4},{6,5},{7,6},{9,8},{10,9},{11,10},{12... | collective-permute-start | bytes 12296 | tf_op jit(solution)/shard_map/ppermute | solution.py:318
  151.5 77.2 %collective-permute-start.9 = (f32[4,256]{1,0:T(4,128)S(1)}, f32[4,256]{1,0:T(4,128)S(1)}, u32[]{:S(2)}, u32[]{:S(2)}) collective-permute-start(f32[4,256]{1,0:T(4,128)S(1)} %get-tuple-element.21), channel_id=1, source_target_pairs={{0,1},{1,2},{2,3},{3,4},{4,5},{5,6},{6,7},{8,9},{9,10},{10,11},{11... | collective-permute-start | bytes 12296 | tf_op jit(solution)/shard_map/ppermute | solution.py:317
  155.6 73.1 %copy-start.7 = (bf16[64,4,256]{2,1,0:T(4,128)(2,1)S(1)}, bf16[64,4,256]{2,1,0:T(4,128)(2,1)}, u32[]{:S(2)}) copy-start(bf16[64,4,256]{2,1,0:T(4,128)(2,1)} %param.13) | copy-start | bytes 393220
  219.8 10.9 %collective-permute-start.11 = (f32[5,64,256]{2,1,0:T(8,128)S(1)}, f32[5,64,256]{2,1,0:T(8,128)S(1)}, u32[]{:S(2)}, u32[]{:S(2)}) collective-permute-start(f32[5,64,256]{2,1,0:T(8,128)S(1)} %get-tuple-element.19), channel_id=1, source_target_pairs={{0,8},{8,16},{16,24},{24,32},{32,40},{40,48},{48,56},{56,64},{64,7... | collective-permute-start | bytes 983048 | tf_op jit(solution)/shard_map/ppermute | solution.py:317
  226.7 10.5 %collective-permute-start.12 = (f32[5,64,256]{2,1,0:T(8,128)S(1)}, f32[5,64,256]{2,1,0:T(8,128)S(1)}, u32[]{:S(2)}, u32[]{:S(2)}) collective-permute-start(f32[5,64,256]{2,1,0:T(8,128)S(1)} %get-tuple-element.20), channel_id=1, source_target_pairs={{8,0},{16,8},{24,16},{32,24},{40,32},{48,40},{56,48},{64,56},{72,6... | collective-permute-start | bytes 983048 | tf_op jit(solution)/shard_map/ppermute | solution.py:318

commit v4 on v3

--- a/solution.py
+++ b/solution.py
@@ -10,7 +10,7 @@
 
 time_step = 0.08
 highest = lax.Precision.HIGHEST
-chips = ("zl", "xx", "zh", "yy")
+chips = ("zl", "zh", "xx", "yy")
 slab = ("zl", "xx", "co")
 grp = ("zh", "yy")
 swap = [(0, 1), (1, 0)]
@@ -54,7 +54,9 @@
 
 def z_of(k, which, half, z_rows):
     groups = half // z_rows
-    return (k % groups) * (2 * z_rows) + which * z_rows + k // groups
+    depth = lax.axis_size("zl")
+    group = (k % groups) % depth * (groups // depth) + (k % groups) // depth
+    return group * (2 * z_rows) + which * z_rows + k // groups
 
 
 def push_plane(marker_x, marker_z, marker_y, drag_weight, inv_y, x_rows, z_rows):
@@ -99,14 +101,20 @@
     lane = lax.broadcasted_iota(jnp.int32, (32, 128), 1)
     low_half = lane < 64
 
+    def messages(zh, yy, depth, row):
+        return [pl.ds((zh * 16 + xx * 4 + yy) * depth + row, 8, stride=32 * depth) for xx in range(4)]
+
+    def put(zh, yy, row, value):
+        for i, at in enumerate(messages(zh, yy, out_rows, row)):
+            out_ref[at, :] = value[8 * i : 8 * i + 8]
+
     def lines(ref, c):
         evens, odds = [None, None], [None, None]
         for pair in range(2):
             even, odd = [], []
             for q in range(4):
-                at = q * rows + 2 * c + pair
-                first = ref[pl.ds(at, 32, stride=8 * rows), :]
-                second = ref[pl.ds(at + 4 * rows, 32, stride=8 * rows), :]
+                first = jnp.concatenate([ref[at, :] for at in messages(0, q, rows, 2 * c + pair)], axis=0)
+                second = jnp.concatenate([ref[at, :] for at in messages(1, q, rows, 2 * c + pair)], axis=0)
                 even.append(jnp.where(low_half, first, pltpu.roll(second, 64, 1)))
                 odd.append(jnp.where(low_half, pltpu.roll(first, 64, 1), second))
             evens[pair] = jnp.concatenate(even, axis=1)
@@ -126,11 +134,10 @@
         for pair in range(2):
             for q in range(4):
                 two = [done[(2 * pair + i) * 32 : (2 * pair + i + 1) * 32, q * 128 : q * 128 + 128] for i in range(2)]
-                at = q * out_rows + 2 * c + pair
                 first = jnp.where(low_half, two[0], pltpu.roll(two[1], 64, 1))
                 second = jnp.where(low_half, pltpu.roll(two[0], 64, 1), two[1])
-                out_ref[pl.ds(at, 32, stride=8 * out_rows), :] = first
-                out_ref[pl.ds(at + 4 * out_rows, 32, stride=8 * out_rows), :] = second
+                put(0, q, 2 * c + pair, first)
+                put(1, q, 2 * c + pair, second)
                 for i in range(2):
                     k = c * 4 + 2 * pair + i
                     outer = pltpu.roll(two[i], 2 * k + 1, 1)
@@ -144,7 +151,7 @@
                         if 0 <= target < 8:
                             edge_ref[target] = jnp.where(lane == spot, value, edge_ref[target])
     for g in range(8):
-        out_ref[pl.ds(g * out_rows + out_rows - 1, 32, stride=8 * out_rows), :] = edge_ref[g]
+        put(g // 4, g % 4, out_rows - 1, edge_ref[g])
 
 
 vmem = pl.BlockSpec(memory_space=pltpu.VMEM)

time: 239 us -> 240 us (level)
  the two profiles are of different devices: /device:TPU:7 before, /device:TPU:103 now
where the time goes in v4:
time: 240 us; the launch traced here: 239 us
  waiting for transfers between devices  128 us (53%)
  starting transfers between devices  83.4 us (35%)
  local copies, waits for them, and re-layouts  11.2 us (5%)
  Pallas kernels  9.5 us (4%)
  matrix products  5.04 us (2%)
    all_to_all x2, waiting for transfers between devices, transposed(): return lax.all_to_all(sent, chips, split_axis=0, concat_axis=0, tiled=True)  63.9 us
    ppermute x1, waiting for transfers between devices, inv_x_pair(): theirs = lax.ppermute(mine, 'zh', swap)  52.4 us
    all_to_all x2, starting transfers between devices, transposed(): return lax.all_to_all(sent, chips, split_axis=0, concat_axis=0, tiled=True)  34.6 us
    ppermute x7, starting transfers between devices, gather_ring(): lax.ppermute(block, axis, [(i, (i + hop) % count) for i in range(count)])  20.4 us
    ppermute x2, starting transfers between devices, before_and_after(): before = lax.ppermute(tail, axes, [(i, i + 1) for i in range(count - 1)])  9.58 us
    ppermute x1, starting transfers between devices, inv_x_pair(): theirs = lax.ppermute(mine, 'zh', swap)  9.21 us
    ppermute x2, waiting for transfers between devices, before_and_after(): after = lax.ppermute(head, axes, [(i + 1, i) for i in range(count - 1)])  7.72 us
    ppermute x1, starting transfers between devices, body(): other = lax.ppermute(got, 'co', swap)  6.39 us
  transfers between devices with their start and end apart: 15, of which 5 were waited for; matrix products, arithmetic and copies ran while one was open for 6% of the time, Pallas kernels for 1%

profile of v4, /device:TPU:103, one launch (start us, length us, event | category | flops | bytes accessed | tf_op | source)
XLA Modules:
  0.0 238.9 jit_solution(16081486150660398139)
XLA Ops:
  0.0 1.4 copy-done.2
  1.4 0.9 copy-done.3
  2.3 2.3 shard_map.109
  4.6 22.3 %all-to-all-start = ((f32[256,1,1280]{2,1,0:T(1,128)}), f32[256,1,1280]{2,1,0:T(1,128)S(1)}, u32[]{:S(2)}, u32[]{:S(2)}) async-start(f32[256,1,1280]{2,1,0:T(1,128)} %bitcast.3), calls=%async_computation | async-start | bytes 2621440 | tf_op jit(solution)/shard_map/all_to_all | solution.py:330
  27.1 9.2 %collective-permute-start.1 = (f32[64,64]{0,1:T(8,128)S(1)}, f32[64,64]{0,1:T(8,128)S(1)}, u32[]{:S(2)}, u32[]{:S(2)}) collective-permute-start(f32[64,64]{0,1:T(8,128)S(1)} %constant_dynamic-slice_fusion), channel_id=1, source_target_pairs={{0,4},{4,0},{1,5},{5,1},{2,6},{6,2},{3,7},{7,3},{8,12},{12,8},{9,1... | collective-permute-start | bytes 49160 | tf_op jit(solution)/shard_map/ppermute | solution.py:44
  36.5 1.0 fusion.8
  39.0 52.4 %collective-permute-done.1 = f32[64,64]{0,1:T(8,128)S(1)} collective-permute-done((f32[64,64]{0,1:T(8,128)S(1)}, f32[64,64]{0,1:T(8,128)S(1)}, u32[]{:S(2)}, u32[]{:S(2)}) %collective-permute-start.1) | collective-permute-done | bytes 16416 | tf_op jit(solution)/shard_map/ppermute | solution.py:44
  91.6 1.9 collective-permute-start.2
  93.5 3.9 %collective-permute-start.3 = (f32[64,128]{0,1:T(8,128)S(1)}, f32[64,128]{0,1:T(8,128)S(1)}, u32[]{:S(2)}, u32[]{:S(2)}) collective-permute-start(f32[64,128]{0,1:T(8,128)S(1)} %get-tuple-element.23), channel_id=1, source_target_pairs={{0,32},{16,48},{32,0},{48,16},{1,33},{17,49},{33,1},{49,17},{2,34}... | collective-permute-start | bytes 98312 | tf_op jit(solution)/shard_map/ppermute | solution.py:35
  97.4 1.9 collective-permute-start.4
  100.8 2.8 %collective-permute-done.4 = f32[64,128]{0,1:T(8,128)S(1)} collective-permute-done((f32[64,128]{0,1:T(8,128)S(1)}, f32[64,128]{0,1:T(8,128)S(1)}, u32[]{:S(2)}, u32[]{:S(2)}) %collective-permute-start.4) | collective-permute-done | bytes 32800 | tf_op jit(solution)/shard_map/ppermute | solution.py:35
  105.5 3.3 %collective-permute-start.5 = (f32[4,64,128]{2,1,0:T(8,128)}, f32[4,64,128]{2,1,0:T(8,128)S(1)}, u32[]{:S(2)}, u32[]{:S(2)}) collective-permute-start(f32[4,64,128]{2,1,0:T(8,128)} %constant_dynamic-update-slice_fusion), channel_id=1, source_target_pairs={{0,1},{1,2},{2,3},{3,0},{4,5},{5,6},{6,7},{7,4},{8,9},{9,10},{10,1... | collective-permute-start | bytes 393224 | tf_op jit(solution)/shard_map/ppermute | solution.py:35
  108.8 4.4 %collective-permute-start.6 = (f32[4,64,128]{2,1,0:T(8,128)}, f32[4,64,128]{2,1,0:T(8,128)}, u32[]{:S(2)}, u32[]{:S(2)}) collective-permute-start(f32[4,64,128]{2,1,0:T(8,128)} %constant_dynamic-update-slice_fusion), channel_id=1, source_target_pairs={{0,2},{1,3},{2,0},{3,1},{4,6},{5,7},{6,4},{7,5},{8,10},{9,11},{10,... | collective-permute-start | bytes 393224 | tf_op jit(solution)/shard_map/ppermute | solution.py:35
  113.2 2.9 %collective-permute-start.7 = (f32[4,64,128]{2,1,0:T(8,128)}, f32[4,64,128]{2,1,0:T(8,128)}, u32[]{:S(2)}, u32[]{:S(2)}) collective-permute-start(f32[4,64,128]{2,1,0:T(8,128)} %constant_dynamic-update-slice_fusion), channel_id=1, source_target_pairs={{0,3},{1,0},{2,1},{3,2},{4,7},{5,4},{6,5},{7,6},{8,11},{9,8},{10,9... | collective-permute-start | bytes 393224 | tf_op jit(solution)/shard_map/ppermute | solution.py:35
  116.2 0.9 bitcast_dynamic-update-slice_fusion.5
  117.2 6.4 %collective-permute-start = (f32[2560,128]{1,0:T(8,128)S(1)}, f32[2560,128]{1,0:T(8,128)S(1)}, u32[]{:S(2)}, u32[]{:S(2)}) collective-permute-start(f32[2560,128]{1,0:T(8,128)S(1)} %bitcast.49), channel_id=1, source_target_pairs={{0,8},{8,0},{1,9},{9,1},{2,10},{10,2},{3,11},{11,3},{4,12},{12,4},... | collective-permute-start | bytes 3932168 | tf_op jit(solution)/shard_map/ppermute | solution.py:358
  123.6 0.9 bitcast_dynamic-update-slice_fusion.3
  124.5 0.9 bitcast_dynamic-update-slice_fusion.2
  125.4 2.1 collective-permute-start.8
  128.1 3.4 %fusion.push_ref = f32[256,512]{1,0:T(8,128)S(1)} fusion(f32[2048]{0:T(1024)S(1)} %mul.102, s32[512]{0:T(512)} %fusion.32, s32[2048]{0:T(1024)} %param.15, s32[2048]{0:T(1024)} %param.16, s32[256]{0:T(256)} %compare_select_fusion), kind=kOutput, calls=%fused_computation | convolution fusion | flops 3223846912 | bytes 551936 | tf_op jit(solution)/shard_map/dot_general | solution.py:79
  131.7 1.1 bitcast_dynamic-update-slice_fusion
  133.0 3.9 %shard_map.111 = f32[2816,128]{1,0:T(8,128)S(1)} custom-call(f32[2560,128]{1,0:T(8,128)S(1)} %bitcast.50, f32[2560,128]{1,0:T(8,128)S(1)} %collective-permute-done.other_ref, f32[256,512]{1,0:T(8,128)S(1)} %fusion.push_ref, bf16[128,256]{1,0:T(8,128)(2,1)S(1)} %get-tuple-element.13.wz_high, bf16[128,256]{1,0:T(8,128)(2,1)S(1)} %get-tuple-element.14.wz_low, ...), custom_call_target="tpu_custom_call" | custom-call | flops 1509949440 | bytes 8388608 | tf_op jit(solution)/shard_map/pallas_call | solution.py:162
  136.9 1.1 copy-done.1
  138.0 12.3 %all-to-all-start.1 = ((f32[256,1,1408]{2,1,0:T(1,128)}), f32[256,1,1408]{2,1,0:T(1,128)S(1)}, u32[]{:S(2)}, u32[]{:S(2)}) async-start(f32[256,1,1408]{2,1,0:T(1,128)} %bitcast.48), calls=%async_computation.1 | async-start | bytes 2883584 | tf_op jit(solution)/shard_map/all_to_all | solution.py:330
  150.3 1.3 collective-permute-start.10
  151.6 4.0 %collective-permute-start.9 = (f32[4,256]{1,0:T(4,128)S(1)}, f32[4,256]{1,0:T(4,128)S(1)}, u32[]{:S(2)}, u32[]{:S(2)}) collective-permute-start(f32[4,256]{1,0:T(4,128)S(1)} %get-tuple-element.21), channel_id=1, source_target_pairs={{0,1},{1,2},{2,3},{3,4},{4,5},{5,6},{6,7},{8,9},{9,10},{10,11},{11... | collective-permute-start | bytes 12296 | tf_op jit(solution)/shard_map/ppermute | solution.py:324
  155.8 63.9 %all-to-all-done.1 = f32[256,1,1408]{2,1,0:T(1,128)S(1)} async-done(((f32[256,1,1408]{2,1,0:T(1,128)}), f32[256,1,1408]{2,1,0:T(1,128)S(1)}, u32[]{:S(2)}, u32[]{:S(2)}) %all-to-all-start.1) | async-done | bytes 1441824 | tf_op jit(solution)/shard_map/all_to_all | solution.py:330
  220.1 5.6 %collective-permute-start.11 = (f32[5,64,256]{2,1,0:T(8,128)S(1)}, f32[5,64,256]{2,1,0:T(8,128)S(1)}, u32[]{:S(2)}, u32[]{:S(2)}) collective-permute-start(f32[5,64,256]{2,1,0:T(8,128)S(1)} %get-tuple-element.19), channel_id=1, source_target_pairs={{0,8},{8,16},{16,24},{24,32},{32,40},{40,48},{48,56},{56,64},{64,7... | collective-permute-start | bytes 983048 | tf_op jit(solution)/shard_map/ppermute | solution.py:324
  225.7 1.9 collective-permute-start.12
  227.7 1.3 shard_map.113.most_ref
  229.7 7.7 %collective-permute-done.12.above_ref = f32[5,64,256]{2,1,0:T(8,128)S(1)} collective-permute-done((f32[5,64,256]{2,1,0:T(8,128)S(1)}, f32[5,64,256]{2,1,0:T(8,128)S(1)}, u32[]{:S(2)}, u32[]{:S(2)}) %collective-permute-start.12) | collective-permute-done | bytes 327712 | tf_op jit(solution)/shard_map/ppermute | solution.py:325
  237.5 1.5 shard_map.114
  (64 shorter events, 7.5 us)
Async XLA Ops:
  0.0 37.8 %copy-start = (f32[256,256]{1,0:T(8,128)S(1)}, f32[256,256]{1,0:T(8,128)}, u32[]{:S(2)}) copy-start(f32[256,256]{1,0:T(8,128)} %param.21) | copy-start | bytes 786436
  0.0 1.4 copy-start.2
  1.4 0.9 copy-start.3
  4.6 22.4 %copy-start.8 = (f32[512,64]{0,1:T(8,128)S(1)}, f32[512,64]{0,1:T(8,128)}, u32[]{:S(2)}) copy-start(f32[512,64]{0,1:T(8,128)} %param.19) | copy-start | bytes 393220
  4.6 31.7 %copy-start.4 = (f32[256,256]{1,0:T(8,128)S(1)}, f32[256,256]{1,0:T(8,128)}, u32[]{:S(2)}) copy-start(f32[256,256]{1,0:T(8,128)} %inv_ref.1) | copy-start | bytes 786436
  4.6 31.9 %copy-start.10 = (s32[2048]{0:T(1024)S(1)}, s32[2048]{0:T(1024)}, u32[]{:S(2)}) copy-start(s32[2048]{0:T(1024)} %param.17) | copy-start | bytes 24580
  4.6 112.5 %all-to-all-start = ((f32[256,1,1280]{2,1,0:T(1,128)}), f32[256,1,1280]{2,1,0:T(1,128)S(1)}, u32[]{:S(2)}, u32[]{:S(2)}) async-start(f32[256,1,1280]{2,1,0:T(1,128)} %bitcast.3), calls=%async_computation | async-start | bytes 2621440 | tf_op jit(solution)/shard_map/all_to_all | solution.py:330
  27.1 64.4 %collective-permute-start.1 = (f32[64,64]{0,1:T(8,128)S(1)}, f32[64,64]{0,1:T(8,128)S(1)}, u32[]{:S(2)}, u32[]{:S(2)}) collective-permute-start(f32[64,64]{0,1:T(8,128)S(1)} %constant_dynamic-slice_fusion), channel_id=1, source_target_pairs={{0,4},{4,0},{1,5},{5,1},{2,6},{6,2},{3,7},{7,3},{8,12},{12,8},{9,1... | collective-permute-start | bytes 49160 | tf_op jit(solution)/shard_map/ppermute | solution.py:44
  39.0 89.1 %copy-start.9 = (f32[2048]{0:T(1024)S(1)}, f32[2048]{0:T(1024)}, u32[]{:S(2)}) copy-start(f32[2048]{0:T(1024)} %param.18) | copy-start | bytes 24580
  91.6 9.1 %collective-permute-start.2 = (f32[64,128]{0,1:T(8,128)S(1)}, f32[64,128]{0,1:T(8,128)S(1)}, u32[]{:S(2)}, u32[]{:S(2)}) collective-permute-start(f32[64,128]{0,1:T(8,128)S(1)} %get-tuple-element.23), channel_id=1, source_target_pairs={{0,16},{16,32},{32,48},{48,0},{1,17},{17,33},{33,49},{49,1},{2,18}... | collective-permute-start | bytes 98312 | tf_op jit(solution)/shard_map/ppermute | solution.py:35
  93.5 7.3 %collective-permute-start.3 = (f32[64,128]{0,1:T(8,128)S(1)}, f32[64,128]{0,1:T(8,128)S(1)}, u32[]{:S(2)}, u32[]{:S(2)}) collective-permute-start(f32[64,128]{0,1:T(8,128)S(1)} %get-tuple-element.23), channel_id=1, source_target_pairs={{0,32},{16,48},{32,0},{48,16},{1,33},{17,49},{33,1},{49,17},{2,34}... | collective-permute-start | bytes 98312 | tf_op jit(solution)/shard_map/ppermute | solution.py:35
  97.4 6.2 %collective-permute-start.4 = (f32[64,128]{0,1:T(8,128)S(1)}, f32[64,128]{0,1:T(8,128)S(1)}, u32[]{:S(2)}, u32[]{:S(2)}) collective-permute-start(f32[64,128]{0,1:T(8,128)S(1)} %get-tuple-element.23), channel_id=1, source_target_pairs={{0,48},{16,0},{32,16},{48,32},{1,49},{17,1},{33,17},{49,33},{2,50}... | collective-permute-start | bytes 98312 | tf_op jit(solution)/shard_map/ppermute | solution.py:35
  105.5 11.6 %collective-permute-start.5 = (f32[4,64,128]{2,1,0:T(8,128)}, f32[4,64,128]{2,1,0:T(8,128)S(1)}, u32[]{:S(2)}, u32[]{:S(2)}) collective-permute-start(f32[4,64,128]{2,1,0:T(8,128)} %constant_dynamic-update-slice_fusion), channel_id=1, source_target_pairs={{0,1},{1,2},{2,3},{3,0},{4,5},{5,6},{6,7},{7,4},{8,9},{9,10},{10,1... | collective-permute-start | bytes 393224 | tf_op jit(solution)/shard_map/ppermute | solution.py:35
  108.8 14.8 %collective-permute-start.6 = (f32[4,64,128]{2,1,0:T(8,128)}, f32[4,64,128]{2,1,0:T(8,128)}, u32[]{:S(2)}, u32[]{:S(2)}) collective-permute-start(f32[4,64,128]{2,1,0:T(8,128)} %constant_dynamic-update-slice_fusion), channel_id=1, source_target_pairs={{0,2},{1,3},{2,0},{3,1},{4,6},{5,7},{6,4},{7,5},{8,10},{9,11},{10,... | collective-permute-start | bytes 393224 | tf_op jit(solution)/shard_map/ppermute | solution.py:35
  113.2 11.3 %collective-permute-start.7 = (f32[4,64,128]{2,1,0:T(8,128)}, f32[4,64,128]{2,1,0:T(8,128)}, u32[]{:S(2)}, u32[]{:S(2)}) collective-permute-start(f32[4,64,128]{2,1,0:T(8,128)} %constant_dynamic-update-slice_fusion), channel_id=1, source_target_pairs={{0,3},{1,0},{2,1},{3,2},{4,7},{5,4},{6,5},{7,6},{8,11},{9,8},{10,9... | collective-permute-start | bytes 393224 | tf_op jit(solution)/shard_map/ppermute | solution.py:35
  117.2 15.8 %collective-permute-start = (f32[2560,128]{1,0:T(8,128)S(1)}, f32[2560,128]{1,0:T(8,128)S(1)}, u32[]{:S(2)}, u32[]{:S(2)}) collective-permute-start(f32[2560,128]{1,0:T(8,128)S(1)} %bitcast.49), channel_id=1, source_target_pairs={{0,8},{8,0},{1,9},{9,1},{2,10},{10,2},{3,11},{11,3},{4,12},{12,4},... | collective-permute-start | bytes 3932168 | tf_op jit(solution)/shard_map/ppermute | solution.py:358
  125.4 6.3 %collective-permute-start.8 = (f32[4,4,64,128]{3,2,1,0:T(8,128)S(1)}, f32[4,4,64,128]{3,2,1,0:T(8,128)}, u32[]{:S(2)}, u32[]{:S(2)}) collective-permute-start(f32[4,4,64,128]{3,2,1,0:T(8,128)S(1)} %bitcast_dynamic-update-slice_fusion.2), channel_id=1, source_target_pairs={{0,8},{8,0},{1,9},{9,1},{2,10},{10,2},{3,11},{11,3},{4,12},{12,4},... | collective-permute-start | bytes 1572872 | tf_op jit(solution)/shard_map/ppermute | solution.py:35
  136.8 1.1 copy-start.1
  138.0 12.3 %copy-start.6 = (s32[64,4,256]{2,1,0:T(4,128)S(1)}, s32[64,4,256]{2,1,0:T(4,128)}, u32[]{:S(2)}) copy-start(s32[64,4,256]{2,1,0:T(4,128)} %param.14) | copy-start | bytes 786436
  138.0 17.7 %copy-start.5 = (bf16[3,64,4,256]{3,2,1,0:T(4,128)(2,1)S(1)}, bf16[3,64,4,256]{3,2,1,0:T(4,128)(2,1)}, u32[]{:S(2)}) copy-start(bf16[3,64,4,256]{3,2,1,0:T(4,128)(2,1)} %param.12) | copy-start | bytes 1179652
  138.0 81.7 %all-to-all-start.1 = ((f32[256,1,1408]{2,1,0:T(1,128)}), f32[256,1,1408]{2,1,0:T(1,128)S(1)}, u32[]{:S(2)}, u32[]{:S(2)}) async-start(f32[256,1,1408]{2,1,0:T(1,128)} %bitcast.48), calls=%async_computation.1 | async-start | bytes 2883584 | tf_op jit(solution)/shard_map/all_to_all | solution.py:330
  150.3 77.4 %collective-permute-start.10 = (f32[4,256]{1,0:T(4,128)S(1)}, f32[4,256]{1,0:T(4,128)S(1)}, u32[]{:S(2)}, u32[]{:S(2)}) collective-permute-start(f32[4,256]{1,0:T(4,128)S(1)} %get-tuple-element.22), channel_id=1, source_target_pairs={{1,0},{2,1},{3,2},{4,3},{5,4},{6,5},{7,6},{9,8},{10,9},{11,10},{12... | collective-permute-start | bytes 12296 | tf_op jit(solution)/shard_map/ppermute | solution.py:325
  151.6 76.1 %collective-permute-start.9 = (f32[4,256]{1,0:T(4,128)S(1)}, f32[4,256]{1,0:T(4,128)S(1)}, u32[]{:S(2)}, u32[]{:S(2)}) collective-permute-start(f32[4,256]{1,0:T(4,128)S(1)} %get-tuple-element.21), channel_id=1, source_target_pairs={{0,1},{1,2},{2,3},{3,4},{4,5},{5,6},{6,7},{8,9},{9,10},{10,11},{11... | collective-permute-start | bytes 12296 | tf_op jit(solution)/shard_map/ppermute | solution.py:324
  155.7 72.0 %copy-start.7 = (bf16[64,4,256]{2,1,0:T(4,128)(2,1)S(1)}, bf16[64,4,256]{2,1,0:T(4,128)(2,1)}, u32[]{:S(2)}) copy-start(bf16[64,4,256]{2,1,0:T(4,128)(2,1)} %param.13) | copy-start | bytes 393220
  220.1 9.6 %collective-permute-start.11 = (f32[5,64,256]{2,1,0:T(8,128)S(1)}, f32[5,64,256]{2,1,0:T(8,128)S(1)}, u32[]{:S(2)}, u32[]{:S(2)}) collective-permute-start(f32[5,64,256]{2,1,0:T(8,128)S(1)} %get-tuple-element.19), channel_id=1, source_target_pairs={{0,8},{8,16},{16,24},{24,32},{32,40},{40,48},{48,56},{56,64},{64,7... | collective-permute-start | bytes 983048 | tf_op jit(solution)/shard_map/ppermute | solution.py:324
  225.7 11.7 %collective-permute-start.12 = (f32[5,64,256]{2,1,0:T(8,128)S(1)}, f32[5,64,256]{2,1,0:T(8,128)S(1)}, u32[]{:S(2)}, u32[]{:S(2)}) collective-permute-start(f32[5,64,256]{2,1,0:T(8,128)S(1)} %get-tuple-element.20), channel_id=1, source_target_pairs={{8,0},{16,8},{24,16},{32,24},{40,32},{48,40},{56,48},{64,56},{72,6... | collective-permute-start | bytes 983048 | tf_op jit(solution)/shard_map/ppermute | solution.py:325
